TPU v7x, 32 devices: a whole 2x2x4 slice. The times are simulated.
32 devices in a mesh: row: 8 (over z, core), col: 4 (over y, x).
Axes of the slice: x: 2, y: 2, z: 4, core: 2. Of those that a mesh axis runs over, the one named last changes fastest.
Arguments:
- tile_values: bfloat16 [2048, 128, 128], P(('row', 'col')), may hold values from -0.1875 to 0.1875
- slot_codes: int32 [2048], P(('row', 'col')), may hold values from -1 to 127, as said below
- right_start: float32 [8192, 256], P(('row', 'col')), may hold values from -6 to 6
- left_start: float32 [8192, 256], P(('row', 'col')), may hold values from -6 to 6
- node_diagonal: float32 [8192], P(('row', 'col')), may hold values from 1 to 3
- row_scale: float32 [8192], P(('row', 'col')), may hold values from 0.2 to 15
Outputs:
- right_block: float32 [8192, 256], P(('row', 'col'))
- left_block: float32 [8192, 256], P(('row', 'col'))
- projections: float32 [2, 256, 256], replicated
Inputs may be any that keep to these rules, and one draw needn't show every extreme that they name: `slot_codes`: slot (s, p, c) carries a tile that device s extracted for owner p; its code is -1 (empty) or a position a 16 + b in p's block grid of 8 x 2 * 8 places. The codes of one owner's live slots over all sources are distinct, so an owner receives at most 32 live tiles, and some owner receives exactly 32. A source fills at most 2 slots for one owner, and some source fills all 2.
All inputs are finite; a program needn't handle non-finite values.
Results may differ from a plain program's by a relative error of at most 0.002.
Values may be sent and summed in bfloat16 or wider, within the bound.
No kernel may reach another device: no remote copies, remote signals or barrier semaphores. Data moves between devices by JAX's collectives and lax.ppermute only.
A program may use at most 128 MiB of HBM per device.

v0:
```python
import jax
import jax.numpy as jnp
from jax import lax
from jax.sharding import PartitionSpec as P

ITERS = 2


epsilon = 1e-06


def local(tile_values, slot_codes, right_start, left_start, node_diagonal, row_scale):
    row_size = lax.axis_size("row")
    col_size = lax.axis_size("col")
    owners = row_size * col_size
    tile_rows = tile_values.shape[1]
    order_rows = right_start.shape[0] * owners
    grid_rows = 2 * col_size
    grid_cols = 2 * row_size
    got_tiles, got_codes = (
        lax.all_to_all(tile_values, ("row", "col"), split_axis=0, concat_axis=0, tiled=True),
        lax.all_to_all(slot_codes, ("row", "col"), split_axis=0, concat_axis=0, tiled=True),
    )
    live = got_codes >= 0
    places = grid_rows * grid_cols
    safe_keys = jnp.where(live, got_codes, places)
    region = jnp.zeros((places, tile_rows, tile_rows), jnp.bfloat16)
    region = region.at[safe_keys].set(got_tiles, mode="drop")
    region = region.reshape(grid_rows, grid_cols, tile_rows, tile_rows).transpose(0, 2, 1, 3)
    matrix = region.reshape(grid_rows * tile_rows, grid_cols * tile_rows)
    scale_col = row_scale[:, None]
    diag_col = node_diagonal[:, None]
    right_vec = right_start
    left_vec = right_start + left_start
    stored = []
    for turn in range(ITERS):
        right_bf = right_vec.astype(jnp.bfloat16)
        scaled_left = scale_col * left_vec
        left_bf = scaled_left.astype(jnp.bfloat16)
        right_cols = lax.all_gather(right_bf, "row", axis=0, tiled=True)
        left_rows = lax.all_gather(left_bf, "col", axis=0, tiled=True)
        right_part = jnp.dot(matrix, right_cols, preferred_element_type=jnp.float32)
        left_part = lax.dot_general(
            matrix, left_rows, (((0,), (0,)), ((), ())), preferred_element_type=jnp.float32
        )
        right_prod = lax.psum_scatter(right_part, "col", scatter_dimension=0, tiled=True)
        left_prod = lax.psum_scatter(left_part, "row", scatter_dimension=0, tiled=True)
        right_new = scale_col * (right_prod + diag_col * right_vec)
        left_new = left_prod + diag_col * scaled_left
        local_proj = jnp.dot(left_vec.T, right_new, precision=lax.Precision.HIGHEST)
        project = lax.psum(local_proj, ("row", "col")) / order_rows
        right_rest = right_new - jnp.dot(right_vec, project, precision=lax.Precision.HIGHEST)
        left_rest = left_new - jnp.dot(left_vec, project.T, precision=lax.Precision.HIGHEST)
        right_sq, left_sq = lax.psum(
            (jnp.sum(right_rest * right_rest, axis=0), jnp.sum(left_rest * left_rest, axis=0)),
            ("row", "col"),
        )
        right_vec = right_rest / jnp.sqrt(right_sq / order_rows + epsilon)[None, :]
        left_vec = left_rest / jnp.sqrt(left_sq / order_rows + epsilon)[None, :]
        stored.append(project)
    return (right_vec, left_vec, jnp.stack(stored))


def solution(mesh):
    return jax.shard_map(
        local,
        mesh=mesh,
        in_specs=(
            P(("row", "col"), None, None),
            P(("row", "col")),
            P(("row", "col"), None),
            P(("row", "col"), None),
            P(("row", "col")),
            P(("row", "col")),
        ),
        out_specs=(P(("row", "col"), None), P(("row", "col"), None), P()),
        check_vma=False,
    )
```

profile of v0, /device:TPU:10, one launch (start us, length us, event | category | flops | bytes accessed | tf_op | source)
XLA Modules:
  0.0 619.3 jit_solution(10229374278468693904)
XLA Ops:
  7.2 0.8 all_to_all.11
  8.0 10.9 %all_to_all.17 = s32[32,2,1]{1,2,0:T(1,128)S(1)} all-to-all(s32[32,2,1]{1,2,0:T(1,128)S(1)} %bitcast.37), channel_id=1, replica_groups=mesh['row'=8,'col'=4] {'row','col'}, dimensions={0} | all-to-all | bytes 512 | tf_op jit(solution)/shard_map/all_to_all | solution.py:22
  18.9 4.8 all-to-all-start.1
  25.9 51.8 %all-to-all-done.1 = bf16[64,128,128]{2,1,0:T(8,128)(2,1)S(1)} async-done(((bf16[64,128,128]{2,1,0:T(8,128)(2,1)}), bf16[64,128,128]{2,1,0:T(8,128)(2,1)S(1)}, u32[]{:S(2)}, u32[]{:S(2)}) %all-to-all-start.1) | async-done | bytes 2097184 | tf_op jit(solution)/shard_map/all_to_all | solution.py:21
  77.7 3.0 broadcast_in_dim.6
  80.7 10.8 %scatter_fusion = bf16[128,128,128]{2,1,0:T(8,128)(2,1)} fusion(bf16[128,128,128]{2,1,0:T(8,128)(2,1)} %broadcast_in_dim.6, s32[64]{0:T(128)S(1)} %fusion.27, bf16[64,128,128]{2,1,0:T(8,128)(2,1)S(1)} %all-to-all-done.1), kind=kCustom, calls=%fused_computation | custom fusion | bytes 6291712 | tf_op jit(solution)/shard_map/scatter | solution.py:28
  91.5 6.8 %copy.11 = bf16[8,16,128,128]{3,1,2,0:T(8,128)(2,1)} copy(bf16[8,16,128,128]{3,2,1,0:T(8,128)(2,1)} %bitcast.32) | data formatting | bytes 8388608 | tf_op jit(solution)/shard_map/reshape | solution.py:29
  98.4 4.7 fusion.6
  103.2 15.2 %all_gather.14 = bf16[1024,256]{1,0:T(8,128)(2,1)S(1)} all-gather(bf16[256,256]{1,0:T(8,128)(2,1)S(1)} %get-tuple-element.7), channel_id=1, replica_groups=mesh['row'=8,'col'=4] {'col'}, dimensions={0}, use_global_device_ids=true | all-gather | bytes 655360 | tf_op jit(solution)/shard_map/all_gather | solution.py:41
  118.4 15.8 %reduce-scatter.5.cloned.1.call-done = f32[256,256]{1,0:T(8,128)} async-done(((f32[1024,256]{1,0:T(8,128)}), f32[256,256]{1,0:T(8,128)}) %reduce-scatter.5.cloned.1.call-update) | async-done | bytes 262160 | tf_op jit(solution)/shard_map/reduce_scatter | solution.py:46
  134.2 2.3 fusion.17
  136.6 5.6 fusion.2
  142.3 124.6 %all-reduce.5.cloned.1.call-done = f32[256,256]{1,0:T(8,128)} async-done(((f32[256,256]{1,0:T(8,128)}), f32[256,256]{1,0:T(8,128)}) %all-reduce.5.cloned.1.call-update) | async-done | bytes 262160 | tf_op jit(solution)/shard_map/psum | solution.py:51
  266.8 1.4 multiply_reduce_fusion.3
  268.2 32.0 %reduce-scatter.9.cloned.1.call-done = f32[256,256]{1,0:T(8,128)} async-done(((f32[2048,256]{1,0:T(8,128)}), f32[256,256]{1,0:T(8,128)}) %reduce-scatter.9.cloned.1.call-update) | async-done | bytes 262160 | tf_op jit(solution)/shard_map/reduce_scatter | solution.py:47
  300.2 1.5 multiply_reduce_fusion.2
  301.7 43.8 %all-reduce.1 = (f32[256]{0:T(256)S(1)}, f32[256]{0:T(256)S(1)}) all-reduce(f32[256]{0:T(256)S(1)} %get-tuple-element.10, f32[256]{0:T(256)S(1)} %get-tuple-element.12), channel_id=1, replica_groups=mesh['row'=8,'col'=4] {'row','col'}, use_global_device_ids=true, to_apply=%region_4.5 | all-reduce | flops 512 | bytes 4096 | tf_op jit(solution)/shard_map/psum | solution.py:54
  346.4 20.5 %all-gather.5.cloned.1.call-done = bf16[2048,256]{1,0:T(8,128)(2,1)} async-done(((bf16[256,256]{1,0:T(8,128)(2,1)}), bf16[2048,256]{1,0:T(8,128)(2,1)}) %all-gather.5.cloned.1.call-update) | async-done | bytes 1048592 | tf_op jit(solution)/shard_map/all_gather | solution.py:40
  366.9 4.7 fusion.4
  371.8 13.6 %all_gather.15 = bf16[1024,256]{1,0:T(8,128)(2,1)S(1)} all-gather(bf16[256,256]{1,0:T(8,128)(2,1)S(1)} %multiply_convert_fusion), channel_id=1, replica_groups=mesh['row'=8,'col'=4] {'col'}, dimensions={0}, use_global_device_ids=true | all-gather | bytes 655360 | tf_op jit(solution)/shard_map/all_gather | solution.py:41
  385.4 14.1 %reduce-scatter.7.cloned.1.call-done = f32[256,256]{1,0:T(8,128)} async-done(((f32[1024,256]{1,0:T(8,128)}), f32[256,256]{1,0:T(8,128)}) %reduce-scatter.7.cloned.1.call-update) | async-done | bytes 262160 | tf_op jit(solution)/shard_map/reduce_scatter | solution.py:46
  399.6 2.3 fusion.18
  402.0 5.6 fusion
  407.6 124.6 %all-reduce.7.cloned.1.call-done = f32[256,256]{1,0:T(8,128)} async-done(((f32[256,256]{1,0:T(8,128)}), f32[256,256]{1,0:T(8,128)}) %all-reduce.7.cloned.1.call-update) | async-done | bytes 262160 | tf_op jit(solution)/shard_map/psum | solution.py:51
  532.2 1.0 multiply_bitcast_fusion
  533.2 0.8 pad_maximum_fusion
  534.0 1.4 multiply_reduce_fusion.1
  535.4 30.5 %reduce-scatter.11.cloned.1.call-done = f32[256,256]{1,0:T(8,128)} async-done(((f32[2048,256]{1,0:T(8,128)}), f32[256,256]{1,0:T(8,128)}) %reduce-scatter.11.cloned.1.call-update) | async-done | bytes 262160 | tf_op jit(solution)/shard_map/reduce_scatter | solution.py:47
  565.9 1.5 multiply_reduce_fusion
  567.4 43.6 %all-reduce = (f32[256]{0:T(256)S(1)}, f32[256]{0:T(256)S(1)}) all-reduce(f32[256]{0:T(256)S(1)} %get-tuple-element.14, f32[256]{0:T(256)S(1)} %get-tuple-element.16), channel_id=1, replica_groups=mesh['row'=8,'col'=4] {'row','col'}, use_global_device_ids=true, to_apply=%region_11.12 | all-reduce | flops 512 | bytes 4096 | tf_op jit(solution)/shard_map/psum | solution.py:54
  611.0 0.7 broadcast_divide_fusion
  611.8 0.7 broadcast_divide_fusion.1
  (42 shorter events, 3.5 us)
Async XLA Ops:
  7.2 16.6 %copy-start.4 = (f32[256]{0:T(256)S(1)}, f32[256]{0:T(256)}, u32[]{:S(2)}) copy-start(f32[256]{0:T(256)} %param.11) | copy-start | bytes 3076
  7.2 16.6 %copy-start.1 = (f32[256,256]{1,0:T(8,128)S(1)}, f32[256,256]{1,0:T(8,128)}, u32[]{:S(2)}) copy-start(f32[256,256]{1,0:T(8,128)} %param.8) | copy-start | bytes 786436
  7.2 16.6 %copy-start.3 = (f32[256,256]{1,0:T(8,128)S(1)}, f32[256,256]{1,0:T(8,128)}, u32[]{:S(2)}) copy-start(f32[256,256]{1,0:T(8,128)} %param.9) | copy-start | bytes 786436
  18.9 58.8 %all-to-all-start.1 = ((bf16[64,128,128]{2,1,0:T(8,128)(2,1)}), bf16[64,128,128]{2,1,0:T(8,128)(2,1)S(1)}, u32[]{:S(2)}, u32[]{:S(2)}) async-start(bf16[64,128,128]{2,1,0:T(8,128)(2,1)} %param.6), calls=%async_computation.1 | async-start | bytes 4194304 | tf_op jit(solution)/shard_map/all_to_all | solution.py:21
  23.7 74.7 %all-gather.3.cloned.1.call-start = ((), (), s32[]{:S(2)}) async-start(), calls=%async_computation.6 | async-start | bytes 1179648 | tf_op jit(solution)/shard_map/all_gather | solution.py:40
  24.5 109.7 %reduce-scatter.5.cloned.1.call-start = ((), (), s32[]{:S(2)}) async-start(), calls=%async_computation.7 | async-start | bytes 1310720 | tf_op jit(solution)/shard_map/reduce_scatter | solution.py:46
  98.4 35.8 %copy-start.5 = (f32[256]{0:T(256)S(1)}, f32[256]{0:T(256)}, u32[]{:S(2)}) copy-start(f32[256]{0:T(256)} %param.10) | copy-start | bytes 3076
  103.1 163.7 %all-reduce.5.cloned.1.call-start = ((), (), s32[]{:S(2)}) async-start(), calls=%async_computation.8 | async-start | bytes 524288 | tf_op jit(solution)/shard_map/psum | solution.py:51
  136.6 130.3 %copy-start.2 = (f32[256,256]{1,0:T(8,128)S(1)}, f32[256,256]{1,0:T(8,128)}, u32[]{:S(2)}) copy-start(f32[256,256]{1,0:T(8,128)} %reduce-scatter.5.cloned.1.call-done) | copy-start | bytes 786436
  136.6 163.7 %reduce-scatter.9.cloned.1.call-start = ((), (), s32[]{:S(2)}) async-start(), calls=%async_computation.11 | async-start | bytes 2359296 | tf_op jit(solution)/shard_map/reduce_scatter | solution.py:47
  142.2 224.7 %all-gather.5.cloned.1.call-start = ((), (), s32[]{:S(2)}) async-start(), calls=%async_computation.9 | async-start | bytes 1179648 | tf_op jit(solution)/shard_map/all_gather | solution.py:40
  346.2 53.4 %reduce-scatter.7.cloned.1.call-start = ((), (), s32[]{:S(2)}) async-start(), calls=%async_computation.10 | async-start | bytes 1310720 | tf_op jit(solution)/shard_map/reduce_scatter | solution.py:46
  371.7 160.5 %all-reduce.7.cloned.1.call-start = ((), (), s32[]{:S(2)}) async-start(), calls=%async_computation.12 | async-start | bytes 524288 | tf_op jit(solution)/shard_map/psum | solution.py:51
  401.9 5.7 copy-start
  401.9 164.0 %reduce-scatter.11.cloned.1.call-start = ((), (), s32[]{:S(2)}) async-start(), calls=%async_computation.13 | async-start | bytes 2359296 | tf_op jit(solution)/shard_map/reduce_scatter | solution.py:47
  407.6 126.5 %copy-start.6 = (f32[256,256]{1,0:T(8,128)S(1)}, f32[256,256]{1,0:T(8,128)}, u32[]{:S(2)}) copy-start(f32[256,256]{1,0:T(8,128)} %reduce-scatter.7.cloned.1.call-done) | copy-start | bytes 786436
Sparse Core Ops, SparseCore 0:
  26.7 30.5 all-gather.2
  103.2 30.9 reduce-scatter.4
  140.3 126.4 all-reduce.4
  269.0 31.2 reduce-scatter.8
  346.3 20.5 all-gather.4
  371.8 27.7 reduce-scatter.6
  405.6 126.5 all-reduce.6
  534.5 31.3 reduce-scatter.10
where the time goes:
time: 621 us; the launch traced here: 619 us
  waiting for transfers between devices  414 us (67%)
  blocking collectives  127 us (20%)
  matrix products  30.9 us (5%)
  local copies, waits for them, and re-layouts  22.1 us (4%)
  between operations  14.3 us (2%)
    psum x2, waiting for transfers between devices, local(): project = lax.psum(local_proj, ('row', 'col')) / order_rows  249 us
    psum x2, blocking collectives, local(): lax.psum((jnp.sum(right_rest * right_rest, axis=0), jnp.sum(left_rest * l...  87.4 us
    reduce_scatter x2, waiting for transfers between devices, local(): lax.psum_scatter(left_part, 'row', scatter_dimension=0, tiled=True)  62.6 us
    all_to_all x1, waiting for transfers between devices, local(): lax.all_to_all(tile_values, ('row', 'col'), split_axis=0, concat_axis=0,...  51.8 us
    reduce_scatter x2, waiting for transfers between devices, local(): lax.psum_scatter(right_part, 'col', scatter_dimension=0, tiled=True)  29.9 us
    all_gather x2, blocking collectives, local(): left_rows = lax.all_gather(left_bf, 'col', axis=0, tiled=True)  28.8 us
    all_gather x2, waiting for transfers between devices, local(): right_cols = lax.all_gather(right_bf, 'row', axis=0, tiled=True)  20.5 us
  transfers between devices with their start and end apart: 9, of which 8 were waited for; matrix products, arithmetic and copies ran while one was open for 6% of the time, Pallas kernels for 0%

commit v1 on v0

--- a/solution.py
+++ b/solution.py
@@ -7,6 +7,22 @@
 
 
 epsilon = 1e-06
+
+
+AXES = ("row", "col")
+
+
+def copies_of_all(piece):
+    owners = lax.axis_size("row") * lax.axis_size("col")
+    copies = jnp.broadcast_to(piece[None], (owners,) + piece.shape)
+    return lax.all_to_all(copies, AXES, split_axis=0, concat_axis=0, tiled=True)
+
+
+def sum_over_all(whole):
+    owners = lax.axis_size("row") * lax.axis_size("col")
+    pieces = whole.reshape(owners, whole.shape[0] // owners, whole.shape[1])
+    piece = jnp.sum(lax.all_to_all(pieces, AXES, split_axis=0, concat_axis=0, tiled=True), axis=0)
+    return copies_of_all(piece).reshape(whole.shape)
 
 
 def local(tile_values, slot_codes, right_start, left_start, node_diagonal, row_scale):
@@ -48,13 +64,11 @@
         right_new = scale_col * (right_prod + diag_col * right_vec)
         left_new = left_prod + diag_col * scaled_left
         local_proj = jnp.dot(left_vec.T, right_new, precision=lax.Precision.HIGHEST)
-        project = lax.psum(local_proj, ("row", "col")) / order_rows
+        project = sum_over_all(local_proj) / order_rows
         right_rest = right_new - jnp.dot(right_vec, project, precision=lax.Precision.HIGHEST)
         left_rest = left_new - jnp.dot(left_vec, project.T, precision=lax.Precision.HIGHEST)
-        right_sq, left_sq = lax.psum(
-            (jnp.sum(right_rest * right_rest, axis=0), jnp.sum(left_rest * left_rest, axis=0)),
-            ("row", "col"),
-        )
+        squares = jnp.stack([jnp.sum(right_rest * right_rest, axis=0), jnp.sum(left_rest * left_rest, axis=0)])
+        right_sq, left_sq = jnp.sum(copies_of_all(squares), axis=0)
         right_vec = right_rest / jnp.sqrt(right_sq / order_rows + epsilon)[None, :]
         left_vec = left_rest / jnp.sqrt(left_sq / order_rows + epsilon)[None, :]
         stored.append(project)

time: 621 us -> 309 us (0.50)
  waiting for transfers between devices: 414 us -> 120 us
  blocking collectives: 127 us -> 97.4 us
  starting transfers between devices: 5.32 us -> 16.3 us
    psum x2 -> x0, waiting for transfers between devices: 249 us -> none  [local(): project = lax.psum(local_proj, ('row', 'col')) / order_rows]
    psum x2 -> x0, blocking collectives: 87.4 us -> none  [local(): lax.psum((jnp.sum(right_rest * right_rest, axis=0), jnp.sum(left_rest * l...]
    all_to_all x0 -> x4, blocking collectives: none -> 60 us  [the longest x2 31.6 us: sum_over_all(): lax.all_to_all(pieces, AXES, split_axis=0, concat_axis=0, tiled=True)]
    reduce_scatter x2, waiting for transfers between devices: 62.6 us -> 10.2 us  [local(): lax.psum_scatter(left_part, 'row', scatter_dimension=0, tiled=True)]
    all_to_all x0 -> x2, waiting for transfers between devices: none -> 16.2 us  [copies_of_all(): return lax.all_to_all(copies, AXES, split_axis=0, concat_axis=0, tiled=True)]
    all_to_all x0 -> x2, starting transfers between devices: none -> 11.1 us  [copies_of_all(): return lax.all_to_all(copies, AXES, split_axis=0, concat_axis=0, tiled=True)]
    reduce_scatter x2, waiting for transfers between devices: 29.9 us -> 20.9 us  [local(): lax.psum_scatter(right_part, 'col', scatter_dimension=0, tiled=True)]
  transfers between devices with their start and end apart: 9 -> 9, of which waited for: 8 -> 8; matrix products, arithmetic and copies ran while one was open for 6% -> 13% of each run, Pallas kernels for 0% -> 0%
where the time goes in v1:
time: 309 us; the launch traced here: 305 us
  waiting for transfers between devices  120 us (39%)
  blocking collectives  97.4 us (32%)
  matrix products  29.6 us (10%)
  local copies, waits for them, and re-layouts  22.8 us (7%)
  starting transfers between devices  16.3 us (5%)
  between operations  14.3 us (5%)
  other arithmetic  4.09 us (1%)
    all_to_all x1, waiting for transfers between devices, local(): lax.all_to_all(tile_values, ('row', 'col'), split_axis=0, concat_axis=0,...  51.8 us
    all_to_all x2, blocking collectives, sum_over_all(): lax.all_to_all(pieces, AXES, split_axis=0, concat_axis=0, tiled=True)  31.6 us
    all_to_all x2, blocking collectives, copies_of_all(): return lax.all_to_all(copies, AXES, split_axis=0, concat_axis=0, tiled=True)  28.4 us
    all_gather x2, blocking collectives, local(): left_rows = lax.all_gather(left_bf, 'col', axis=0, tiled=True)  26.5 us
    reduce_scatter x2, waiting for transfers between devices, local(): lax.psum_scatter(right_part, 'col', scatter_dimension=0, tiled=True)  20.9 us
    all_gather x2, waiting for transfers between devices, local(): right_cols = lax.all_gather(right_bf, 'row', axis=0, tiled=True)  20.8 us
    all_to_all x2, waiting for transfers between devices, copies_of_all(): return lax.all_to_all(copies, AXES, split_axis=0, concat_axis=0, tiled=True)  16.2 us
    dot_general x2, matrix products, local(): lax.dot_general(matrix, left_rows, (((0,), (0,)), ((), ())), preferred_el...  11.3 us
  transfers between devices with their start and end apart: 9, of which 8 were waited for; matrix products, arithmetic and copies ran while one was open for 13% of the time, Pallas kernels for 0%

profile of v1, /device:TPU:10, one launch (start us, length us, event | category | flops | bytes accessed | tf_op | source)
XLA Modules:
  0.0 304.5 jit_solution(3686785995710939175)
XLA Ops:
  8.0 10.9 %all_to_all.47 = s32[32,2,1]{1,2,0:T(1,128)S(1)} all-to-all(s32[32,2,1]{1,2,0:T(1,128)S(1)} %bitcast.67), channel_id=1, replica_groups=mesh['row'=8,'col'=4] {'row','col'}, dimensions={0} | all-to-all | bytes 512 | tf_op jit(solution)/shard_map/all_to_all | solution.py:38
  18.9 4.8 %all-to-all-start.1 = ((bf16[64,128,128]{2,1,0:T(8,128)(2,1)}), bf16[64,128,128]{2,1,0:T(8,128)(2,1)S(1)}, u32[]{:S(2)}, u32[]{:S(2)}) async-start(bf16[64,128,128]{2,1,0:T(8,128)(2,1)} %param.6), calls=%async_computation.1 | async-start | bytes 4194304 | tf_op jit(solution)/shard_map/all_to_all | solution.py:37
  25.9 51.8 %all-to-all-done.1 = bf16[64,128,128]{2,1,0:T(8,128)(2,1)S(1)} async-done(((bf16[64,128,128]{2,1,0:T(8,128)(2,1)}), bf16[64,128,128]{2,1,0:T(8,128)(2,1)S(1)}, u32[]{:S(2)}, u32[]{:S(2)}) %all-to-all-start.1) | async-done | bytes 2097184 | tf_op jit(solution)/shard_map/all_to_all | solution.py:37
  77.7 3.0 broadcast_in_dim.14
  80.7 10.1 %scatter_fusion = bf16[128,128,128]{2,1,0:T(8,128)(2,1)} fusion(bf16[128,128,128]{2,1,0:T(8,128)(2,1)} %broadcast_in_dim.14, s32[64]{0:T(128)S(1)} %fusion.37, bf16[64,128,128]{2,1,0:T(8,128)(2,1)S(1)} %all-to-all-done.1), kind=kCustom, calls=%fused_computation | custom fusion | bytes 6291712 | tf_op jit(solution)/shard_map/scatter | solution.py:44
  90.8 6.8 %copy.15 = bf16[8,16,128,128]{3,1,2,0:T(8,128)(2,1)} copy(bf16[8,16,128,128]{3,2,1,0:T(8,128)(2,1)} %bitcast.62) | data formatting | bytes 8388608 | tf_op jit(solution)/shard_map/reshape | solution.py:45
  97.7 4.7 %fusion.6 = f32[1024,256]{1,0:T(8,128)} fusion(bf16[2048,256]{1,0:T(8,128)(2,1)} %all-gather.3.cloned.1.call-done, bf16[128,8,16,128]{3,2,1,0:T(8,128)(2,1)} %bitcast.63), kind=kOutput, calls=%fused_computation.7 | convolution fusion | flops 1073741824 | bytes 6291456 | tf_op jit(solution)/shard_map/dot_general | solution.py:58
  102.5 13.0 %all_gather.13 = bf16[1024,256]{1,0:T(8,128)(2,1)S(1)} all-gather(bf16[256,256]{1,0:T(8,128)(2,1)S(1)} %get-tuple-element.3), channel_id=1, replica_groups=mesh['row'=8,'col'=4] {'col'}, dimensions={0}, use_global_device_ids=true | all-gather | bytes 655360 | tf_op jit(solution)/shard_map/all_gather | solution.py:57
  115.5 5.7 %fusion.4 = f32[2048,256]{1,0:T(8,128)} fusion(bf16[1024,256]{1,0:T(8,128)(2,1)S(1)} %all_gather.13, bf16[128,8,16,128]{3,2,1,0:T(8,128)(2,1)} %bitcast.64), kind=kOutput, calls=%fused_computation.5 | convolution fusion | flops 1073741824 | bytes 6815744 | tf_op jit(solution)/shard_map/dot_general | solution.py:59
  121.3 12.4 %reduce-scatter.5.cloned.1.call-done = f32[256,256]{1,0:T(8,128)} async-done(((f32[1024,256]{1,0:T(8,128)}), f32[256,256]{1,0:T(8,128)}) %reduce-scatter.5.cloned.1.call-update) | async-done | bytes 262160 | tf_op jit(solution)/shard_map/reduce_scatter | solution.py:62
  133.7 1.6 convolution_bitcast_fusion.2
  135.3 15.7 %all_to_all.48 = f32[32,8,256]{2,1,0:T(8,128)S(1)} all-to-all(f32[32,8,256]{2,1,0:T(8,128)S(1)} %convolution_bitcast_fusion.2), channel_id=1, replica_groups=mesh['row'=8,'col'=4] {'row','col'}, dimensions={0} | all-to-all | bytes 524288 | tf_op jit(solution)/shard_map/all_to_all | solution.py:24
  151.1 16.6 %all_to_all.49 = f32[32,8,256]{2,1,0:T(8,128)S(1)} all-to-all(f32[32,8,256]{2,1,0:T(8,128)S(1)} %broadcast_in_dim.16), channel_id=1, replica_groups=mesh['row'=8,'col'=4] {'row','col'}, dimensions={0} | all-to-all | bytes 524288 | tf_op jit(solution)/shard_map/all_to_all | solution.py:18
  167.8 1.4 multiply_reduce_fusion.3
  169.1 5.3 %reduce-scatter.7.cloned.1.call-done = f32[256,256]{1,0:T(8,128)} async-done(((f32[2048,256]{1,0:T(8,128)}), f32[256,256]{1,0:T(8,128)}) %reduce-scatter.7.cloned.1.call-update) | async-done | bytes 262160 | tf_op jit(solution)/shard_map/reduce_scatter | solution.py:63
  174.4 1.4 multiply_reduce_fusion.2
  175.8 11.7 %all_to_all.50 = f32[32,2,256]{2,1,0:T(2,128)S(1)} all-to-all(f32[32,2,256]{2,1,0:T(2,128)S(1)} %broadcast_in_dim.17), channel_id=1, replica_groups=mesh['row'=8,'col'=4] {'row','col'}, dimensions={0} | all-to-all | bytes 131072 | tf_op jit(solution)/shard_map/all_to_all | solution.py:18
  188.5 20.8 %all-gather.5.cloned.1.call-done = bf16[2048,256]{1,0:T(8,128)(2,1)} async-done(((bf16[256,256]{1,0:T(8,128)(2,1)}), bf16[2048,256]{1,0:T(8,128)(2,1)}) %all-gather.5.cloned.1.call-update) | async-done | bytes 1048592 | tf_op jit(solution)/shard_map/all_gather | solution.py:56
  209.4 4.7 %fusion.2 = f32[1024,256]{1,0:T(8,128)} fusion(bf16[2048,256]{1,0:T(8,128)(2,1)} %all-gather.5.cloned.1.call-done, bf16[128,8,16,128]{3,2,1,0:T(8,128)(2,1)} %bitcast.65), kind=kOutput, calls=%fused_computation.3 | convolution fusion | flops 1073741824 | bytes 6291456 | tf_op jit(solution)/shard_map/dot_general | solution.py:58
  214.3 13.5 %all_gather.15 = bf16[1024,256]{1,0:T(8,128)(2,1)S(1)} all-gather(bf16[256,256]{1,0:T(8,128)(2,1)S(1)} %multiply_convert_fusion), channel_id=1, replica_groups=mesh['row'=8,'col'=4] {'col'}, dimensions={0}, use_global_device_ids=true | all-gather | bytes 655360 | tf_op jit(solution)/shard_map/all_gather | solution.py:57
  227.8 5.6 %fusion = f32[2048,256]{1,0:T(8,128)} fusion(bf16[1024,256]{1,0:T(8,128)(2,1)S(1)} %all_gather.15, bf16[128,8,16,128]{3,2,1,0:T(8,128)(2,1)} %bitcast.66), kind=kOutput, calls=%fused_computation.1 | convolution fusion | flops 1073741824 | bytes 6815744 | tf_op jit(solution)/shard_map/dot_general | solution.py:59
  233.5 8.5 %reduce-scatter.9.cloned.1.call-done = f32[256,256]{1,0:T(8,128)} async-done(((f32[1024,256]{1,0:T(8,128)}), f32[256,256]{1,0:T(8,128)}) %reduce-scatter.9.cloned.1.call-update) | async-done | bytes 262160 | tf_op jit(solution)/shard_map/reduce_scatter | solution.py:62
  242.0 1.6 convolution_bitcast_fusion
  243.7 15.9 %all_to_all.51 = f32[32,8,256]{2,1,0:T(8,128)S(1)} all-to-all(f32[32,8,256]{2,1,0:T(8,128)S(1)} %convolution_bitcast_fusion), channel_id=1, replica_groups=mesh['row'=8,'col'=4] {'row','col'}, dimensions={0} | all-to-all | bytes 524288 | tf_op jit(solution)/shard_map/all_to_all | solution.py:24
  260.3 4.8 %all-to-all-start.6 = ((f32[32,8,256]{2,1,0:T(8,128)}), f32[32,8,256]{2,1,0:T(8,128)S(1)}, u32[]{:S(2)}, u32[]{:S(2)}) async-start(f32[32,8,256]{2,1,0:T(8,128)} %broadcast_in_dim.18), calls=%async_computation.9 | async-start | bytes 524288 | tf_op jit(solution)/shard_map/all_to_all | solution.py:18
  265.1 11.7 %all-to-all-done.6 = f32[32,8,256]{2,1,0:T(8,128)S(1)} async-done(((f32[32,8,256]{2,1,0:T(8,128)}), f32[32,8,256]{2,1,0:T(8,128)S(1)}, u32[]{:S(2)}, u32[]{:S(2)}) %all-to-all-start.6) | async-done | bytes 262176 | tf_op jit(solution)/shard_map/all_to_all | solution.py:18
  276.8 1.4 multiply_reduce_fusion.1
  278.2 4.9 %reduce-scatter.11.cloned.1.call-done = f32[256,256]{1,0:T(8,128)} async-done(((f32[2048,256]{1,0:T(8,128)}), f32[256,256]{1,0:T(8,128)}) %reduce-scatter.11.cloned.1.call-update) | async-done | bytes 262160 | tf_op jit(solution)/shard_map/reduce_scatter | solution.py:63
  283.1 1.4 multiply_reduce_fusion
  285.2 6.3 %all-to-all-start.7 = ((f32[32,2,256]{2,1,0:T(2,128)}), f32[32,2,256]{2,1,0:T(2,128)S(1)}, u32[]{:S(2)}, u32[]{:S(2)}) async-start(f32[32,2,256]{2,1,0:T(2,128)} %broadcast_in_dim.19), calls=%async_computation.11 | async-start | bytes 131072 | tf_op jit(solution)/shard_map/all_to_all | solution.py:18
  292.3 4.4 %all-to-all-done.7 = f32[32,2,256]{2,1,0:T(2,128)S(1)} async-done(((f32[32,2,256]{2,1,0:T(2,128)}), f32[32,2,256]{2,1,0:T(2,128)S(1)}, u32[]{:S(2)}, u32[]{:S(2)}) %all-to-all-start.7) | async-done | bytes 65568 | tf_op jit(solution)/shard_map/all_to_all | solution.py:18
  296.8 0.8 broadcast_divide_fusion
  (44 shorter events, 6.6 us)
Async XLA Ops:
  7.2 16.6 %copy-start.2 = (f32[256]{0:T(256)S(1)}, f32[256]{0:T(256)}, u32[]{:S(2)}) copy-start(f32[256]{0:T(256)} %param.11) | copy-start | bytes 3076
  7.2 16.6 %copy-start = (f32[256,256]{1,0:T(8,128)S(1)}, f32[256,256]{1,0:T(8,128)}, u32[]{:S(2)}) copy-start(f32[256,256]{1,0:T(8,128)} %param.8) | copy-start | bytes 786436
  7.2 16.6 %copy-start.1 = (f32[256,256]{1,0:T(8,128)S(1)}, f32[256,256]{1,0:T(8,128)}, u32[]{:S(2)}) copy-start(f32[256,256]{1,0:T(8,128)} %param.9) | copy-start | bytes 786436
  18.9 58.8 %all-to-all-start.1 = ((bf16[64,128,128]{2,1,0:T(8,128)(2,1)}), bf16[64,128,128]{2,1,0:T(8,128)(2,1)S(1)}, u32[]{:S(2)}, u32[]{:S(2)}) async-start(bf16[64,128,128]{2,1,0:T(8,128)(2,1)} %param.6), calls=%async_computation.1 | async-start | bytes 4194304 | tf_op jit(solution)/shard_map/all_to_all | solution.py:37
  23.7 74.0 %all-gather.3.cloned.1.call-start = ((), (), s32[]{:S(2)}) async-start(), calls=%async_computation.12 | async-start | bytes 1179648 | tf_op jit(solution)/shard_map/all_gather | solution.py:56
  24.5 109.1 %reduce-scatter.5.cloned.1.call-start = ((), (), s32[]{:S(2)}) async-start(), calls=%async_computation.13 | async-start | bytes 1310720 | tf_op jit(solution)/shard_map/reduce_scatter | solution.py:62
  102.4 72.0 %reduce-scatter.7.cloned.1.call-start = ((), (), s32[]{:S(2)}) async-start(), calls=%async_computation.14 | async-start | bytes 2359296 | tf_op jit(solution)/shard_map/reduce_scatter | solution.py:63
  115.5 18.2 %copy-start.3 = (f32[256]{0:T(256)S(1)}, f32[256]{0:T(256)}, u32[]{:S(2)}) copy-start(f32[256]{0:T(256)} %param.10) | copy-start | bytes 3076
  121.2 88.1 %all-gather.5.cloned.1.call-start = ((), (), s32[]{:S(2)}) async-start(), calls=%async_computation.15 | async-start | bytes 1179648 | tf_op jit(solution)/shard_map/all_gather | solution.py:56
  188.3 53.7 %reduce-scatter.9.cloned.1.call-start = ((), (), s32[]{:S(2)}) async-start(), calls=%async_computation.16 | async-start | bytes 1310720 | tf_op jit(solution)/shard_map/reduce_scatter | solution.py:62
  214.1 69.0 %reduce-scatter.11.cloned.1.call-start = ((), (), s32[]{:S(2)}) async-start(), calls=%async_computation.17 | async-start | bytes 2359296 | tf_op jit(solution)/shard_map/reduce_scatter | solution.py:63
  260.3 16.5 %all-to-all-start.6 = ((f32[32,8,256]{2,1,0:T(8,128)}), f32[32,8,256]{2,1,0:T(8,128)S(1)}, u32[]{:S(2)}, u32[]{:S(2)}) async-start(f32[32,8,256]{2,1,0:T(8,128)} %broadcast_in_dim.18), calls=%async_computation.9 | async-start | bytes 524288 | tf_op jit(solution)/shard_map/all_to_all | solution.py:18
  285.2 11.6 %all-to-all-start.7 = ((f32[32,2,256]{2,1,0:T(2,128)}), f32[32,2,256]{2,1,0:T(2,128)S(1)}, u32[]{:S(2)}, u32[]{:S(2)}) async-start(f32[32,2,256]{2,1,0:T(2,128)} %broadcast_in_dim.19), calls=%async_computation.11 | async-start | bytes 131072 | tf_op jit(solution)/shard_map/all_to_all | solution.py:18
Sparse Core Ops, SparseCore 0:
  26.7 30.5 all-gather.2
  102.6 31.0 reduce-scatter.4
  135.9 38.3 reduce-scatter.6
  188.4 20.9 all-gather.4
  214.3 27.7 reduce-scatter.8
  244.2 38.9 reduce-scatter.10

commit v2 on v1

v2 whole, which is shorter than its diff:
```python
import jax
import jax.numpy as jnp
from jax import lax
from jax.experimental import pallas as pl
from jax.experimental.pallas import tpu as pltpu
from jax.sharding import PartitionSpec as P


ITERS = 2
AXES = ("row", "col")

epsilon = 1e-06
bf16 = jnp.bfloat16
f32 = jnp.float32
FIRST = (((0,), (0,)), ((), ()))


def partner(value, axis, offset):
    size = lax.axis_size(axis)
    return lax.ppermute(value, axis, [(index, index ^ offset) for index in range(size)])


def copies_of_all(piece):
    owners = lax.axis_size("row") * lax.axis_size("col")
    copies = jnp.broadcast_to(piece[None], (owners,) + piece.shape)
    return lax.all_to_all(copies, AXES, split_axis=0, concat_axis=0, tiled=True)


def sum_over_all(whole):
    owners = lax.axis_size("row") * lax.axis_size("col")
    pieces = whole.reshape(owners, whole.shape[0] // owners, whole.shape[1])
    slices = lax.all_to_all(pieces, AXES, split_axis=0, concat_axis=0, tiled=True)
    piece = jnp.sum(slices, axis=0)
    return copies_of_all(piece).reshape(whole.shape)


def assemble(tiles, codes, place, levels, col_size):
    slots, tile, _ = tiles.shape
    grid_cols = 4 * levels
    cap = slots // (2 * levels * col_size)
    shape = jax.ShapeDtypeStruct((2 * col_size * tile, 2 * levels * tile), tiles.dtype)

    def kernel(code_ref, place_ref, tile_ref, own_ref, sib_ref):
        level, core, col = place_ref[0], place_ref[1], place_ref[2]
        me = (level * 2 + core) * col_size + col
        own_ref[...] = jnp.zeros_like(own_ref)
        sib_ref[...] = jnp.zeros_like(sib_ref)

        def put(slot, carry):
            source = slot // cap
            source_row = source // col_size
            near = ((source_row // 2) ^ level) * 2 + ((source_row % 2) ^ core)
            near = near * col_size + ((source % col_size) ^ col)
            code = code_ref[near * slots + me * cap + slot % cap]

            @pl.when(code >= 0)
            def _():
                block_row = code // grid_cols
                block_col = code % grid_cols
                owner_row = block_col // 2
                down = ((block_row // 2) ^ col) * 2 + block_row % 2
                across = ((owner_row // 2) ^ level) * 2 + block_col % 2
                rows = pl.ds(pl.multiple_of(down * tile, tile), tile)
                cols = pl.ds(pl.multiple_of(across * tile, tile), tile)

                @pl.when(owner_row % 2 == core)
                def _():
                    own_ref[rows, cols] = tile_ref[slot]

                @pl.when(owner_row % 2 != core)
                def _():
                    sib_ref[rows, cols] = tile_ref[slot]

            return carry

        lax.fori_loop(0, slots, put, 0)

    return pl.pallas_call(
        kernel,
        out_shape=(shape, shape),
        in_specs=[
            pl.BlockSpec(memory_space=pltpu.SMEM),
            pl.BlockSpec(memory_space=pltpu.SMEM),
            pl.BlockSpec(memory_space=pltpu.VMEM),
        ],
        name="assemble",
    )(codes, place, tiles)


def project_part(left, right, extra):
    rows, ports = left[0].shape

    def kernel(*refs):
        lefts, rights, extra_ref, out_ref = refs[:2], refs[2:4], refs[4], refs[5]
        total = extra_ref[...]
        for left_ref, right_ref in zip(lefts, rights):
            for start in range(0, rows, ports):
                part = right_ref[start : start + ports]
                high = part.astype(bf16)
                low = (part - high.astype(f32)).astype(bf16)
                weight = left_ref[start : start + ports]
                total += lax.dot_general(weight, high, FIRST, preferred_element_type=f32)
                total += lax.dot_general(weight, low, FIRST, preferred_element_type=f32)
        out_ref[...] = total

    return pl.pallas_call(
        kernel, out_shape=jax.ShapeDtypeStruct((ports, ports), f32), name="project_part"
    )(*left, *right, extra)


def local(tile_values, slot_codes, right_start, left_start, node_diagonal, row_scale):
    row_size = lax.axis_size("row")
    col_size = lax.axis_size("col")
    levels = row_size // 2
    rows = right_start.shape[0]
    order_rows = rows * row_size * col_size
    row_index = lax.axis_index("row")
    place = jnp.stack([row_index // 2, row_index % 2, lax.axis_index("col")]).astype(jnp.int32)

    def gather(right, left):
        right_all = jnp.concatenate(
            [right] + [partner(right, "row", 2 * k) for k in range(1, levels)], axis=0
        )
        left_own = jnp.concatenate([left] + [partner(left, "col", k) for k in range(1, col_size)], axis=0)
        return right_all, left_own, partner(left_own, "row", 1)

    scale_col = row_scale[:, None]
    diag_col = node_diagonal[:, None]
    right_vec = right_start
    left_vec = right_start + left_start
    stored = []
    for turn in range(ITERS):
        right_bf = right_vec.astype(bf16)
        scaled_left = scale_col * left_vec
        left_bf = scaled_left.astype(bf16)
        diag_right = diag_col * right_vec
        local_proj = lax.dot_general(scaled_left, diag_right, FIRST, precision=lax.Precision.HIGHEST)
        right_all, left_own, left_sib = gather(right_bf, left_bf)
        if turn == 0:
            got_tiles = lax.all_to_all(tile_values, AXES, split_axis=0, concat_axis=0, tiled=True)
            codes = slot_codes
            for axis, offsets in (
                ("col", range(1, col_size)),
                ("row", (1,)),
                ("row", range(2, row_size, 2)),
            ):
                codes = jnp.concatenate([codes] + [partner(codes, axis, k) for k in offsets])
            got_tiles, codes, right_all, left_own, left_sib = lax.optimization_barrier(
                (got_tiles, codes, right_all, left_own, left_sib)
            )
            own_half, sib_half = assemble(got_tiles, codes, place, levels, col_size)
            other_half = partner(sib_half, "row", 1)
        left_part = lax.dot_general(own_half, left_own, FIRST, preferred_element_type=f32) + lax.dot_general(
            other_half, left_sib, FIRST, preferred_element_type=f32
        )
        left_part, right_all = lax.optimization_barrier((left_part, right_all))
        right_own = jnp.dot(own_half, right_all, preferred_element_type=f32)
        right_sib = jnp.dot(other_half, right_all, preferred_element_type=f32)
        left_prod = left_part[:rows]
        for k in range(1, levels):
            left_prod += partner(left_part[k * rows : (k + 1) * rows], "row", 2 * k)
        project = project_part((left_own, left_sib), (right_own, right_sib), local_proj)
        project = sum_over_all(project) / order_rows
        right_got = partner(right_sib, "row", 1)
        right_pair = right_own + right_got
        right_prod = right_pair[:rows]
        for k in range(1, col_size):
            right_prod += partner(right_pair[k * rows : (k + 1) * rows], "col", k)
        right_new = scale_col * (right_prod + diag_right)
        left_new = left_prod + diag_col * scaled_left
        right_rest = right_new - jnp.dot(right_vec, project, precision=lax.Precision.HIGHEST)
        left_rest = left_new - jnp.dot(left_vec, project.T, precision=lax.Precision.HIGHEST)
        squares = jnp.stack(
            [jnp.sum(right_rest * right_rest, axis=0), jnp.sum(left_rest * left_rest, axis=0)]
        )
        right_sq, left_sq = jnp.sum(copies_of_all(squares), axis=0)
        right_vec = right_rest / jnp.sqrt(right_sq / order_rows + epsilon)[None, :]
        left_vec = left_rest / jnp.sqrt(left_sq / order_rows + epsilon)[None, :]
        stored.append(project)
    return (right_vec, left_vec, jnp.stack(stored))


def solution(mesh):
    return jax.shard_map(
        local,
        mesh=mesh,
        in_specs=(
            P(AXES, None, None),
            P(AXES),
            P(AXES, None),
            P(AXES, None),
            P(AXES),
            P(AXES),
        ),
        out_specs=(P(AXES, None), P(AXES, None), P()),
        check_vma=False,
    )
```

time: 309 us -> 266 us (0.86)
  blocking collectives: 97.4 us -> 24.1 us
  starting transfers between devices: 16.3 us -> 71.2 us
  Pallas kernels: 0 us -> 13.5 us
  between operations: 14.3 us -> 1.11 us
  local copies, waits for them, and re-layouts: 22.8 us -> 11.8 us
  matrix products: 29.6 us -> 19.9 us
  waiting for transfers between devices: 120 us -> 112 us
  other arithmetic: 4.09 us -> 8.3 us
    ppermute x0 -> x36, waiting for transfers between devices: none -> 85 us  [partner(): lax.ppermute(value, axis, [(index, index ^ offset) for index in range(siz...]
    all_to_all x1 -> x2, waiting for transfers between devices: 51.8 us -> 8.52 us  [the longest x1 8.52 us: sum_over_all(): lax.all_to_all(pieces, AXES, split_axis=0, concat_axis=0, tiled=True)]
    ppermute x0 -> x36, starting transfers between devices: none -> 41.3 us  [partner(): lax.ppermute(value, axis, [(index, index ^ offset) for index in range(siz...]
    reduce_scatter x4 -> x0, waiting for transfers between devices: 31.1 us -> none  [the longest x2 20.9 us: local(): lax.psum_scatter(right_part, 'col', scatter_dimension=0, tiled=True)]
    all_gather x2 -> x0, blocking collectives: 26.5 us -> none  [local(): left_rows = lax.all_gather(left_bf, 'col', axis=0, tiled=True)]
    all_gather x2 -> x0, waiting for transfers between devices: 20.8 us -> none  [local(): right_cols = lax.all_gather(right_bf, 'row', axis=0, tiled=True)]
    all_to_all x2 -> x1, blocking collectives: 28.4 us -> 9.22 us  [copies_of_all(): return lax.all_to_all(copies, AXES, split_axis=0, concat_axis=0, tiled=True)]
    all_to_all x2 -> x1, blocking collectives: 31.6 us -> 14.8 us  [sum_over_all(): lax.all_to_all(pieces, AXES, split_axis=0, concat_axis=0, tiled=True)]
  transfers between devices with their start and end apart: 9 -> 41, of which waited for: 8 -> 20; matrix products, arithmetic and copies ran while one was open for 13% -> 9% of each run, Pallas kernels for 0% -> 1%
where the time goes in v2:
time: 266 us; the launch traced here: 262 us
  waiting for transfers between devices  112 us (42%)
  starting transfers between devices  71.2 us (27%)
  blocking collectives  24.1 us (9%)
  matrix products  19.9 us (7%)
  Pallas kernels  13.5 us (5%)
  local copies, waits for them, and re-layouts  11.8 us (4%)
  other arithmetic  8.3 us (3%)
    ppermute x36, waiting for transfers between devices, partner(): lax.ppermute(value, axis, [(index, index ^ offset) for index in range(siz...  85 us
    ppermute x36, starting transfers between devices, partner(): lax.ppermute(value, axis, [(index, index ^ offset) for index in range(siz...  41.3 us
    all_to_all x3, waiting for transfers between devices, copies_of_all(): return lax.all_to_all(copies, AXES, split_axis=0, concat_axis=0, tiled=True)  18.4 us
    all_to_all x1, blocking collectives, sum_over_all(): lax.all_to_all(pieces, AXES, split_axis=0, concat_axis=0, tiled=True)  14.8 us
    all_to_all x3, starting transfers between devices, copies_of_all(): return lax.all_to_all(copies, AXES, split_axis=0, concat_axis=0, tiled=True)  14.3 us
    all_to_all x1, starting transfers between devices, sum_over_all(): lax.all_to_all(pieces, AXES, split_axis=0, concat_axis=0, tiled=True)  9.64 us
    all_to_all x1, blocking collectives, copies_of_all(): return lax.all_to_all(copies, AXES, split_axis=0, concat_axis=0, tiled=True)  9.22 us
    all_to_all x1, waiting for transfers between devices, sum_over_all(): lax.all_to_all(pieces, AXES, split_axis=0, concat_axis=0, tiled=True)  8.52 us
  transfers between devices with their start and end apart: 41, of which 20 were waited for; matrix products, arithmetic and copies ran while one was open for 9% of the time, Pallas kernels for 1%

profile of v2, /device:TPU:10, one launch (start us, length us, event | category | flops | bytes accessed | tf_op | source)
XLA Modules:
  0.0 261.8 jit_solution(6869489799585370397)
XLA Ops:
  0.7 6.0 %all-to-all-start = ((bf16[64,128,128]{2,1,0:T(8,128)(2,1)}), bf16[64,128,128]{2,1,0:T(8,128)(2,1)S(1)}, u32[]{:S(2)}, u32[]{:S(2)}) async-start(bf16[64,128,128]{2,1,0:T(8,128)(2,1)} %param.6), calls=%async_computation | async-start | bytes 4194304 | tf_op jit(solution)/shard_map/all_to_all | solution.py:140
  10.4 15.7 %collective-permute-done.12 = bf16[256,256]{1,0:T(8,128)(2,1)S(1)} collective-permute-done((bf16[256,256]{1,0:T(8,128)(2,1)S(1)}, bf16[256,256]{1,0:T(8,128)(2,1)S(1)}, u32[]{:S(2)}, u32[]{:S(2)}) %collective-permute-start.12) | collective-permute-done | bytes 131104 | tf_op jit(solution)/shard_map/ppermute | solution.py:20
  26.1 3.7 %collective-permute-done.11 = bf16[256,256]{1,0:T(8,128)(2,1)S(1)} collective-permute-done((bf16[256,256]{1,0:T(8,128)(2,1)S(1)}, bf16[256,256]{1,0:T(8,128)(2,1)S(1)}, u32[]{:S(2)}, u32[]{:S(2)}) %collective-permute-start.11) | collective-permute-done | bytes 131104 | tf_op jit(solution)/shard_map/ppermute | solution.py:20
  31.0 2.5 collective-permute-start.2
  33.5 3.1 %collective-permute-start.9 = (bf16[256,256]{1,0:T(8,128)(2,1)S(1)}, bf16[256,256]{1,0:T(8,128)(2,1)S(1)}, u32[]{:S(2)}, u32[]{:S(2)}) collective-permute-start(bf16[256,256]{1,0:T(8,128)(2,1)S(1)} %get-tuple-element.41), channel_id=1, source_target_pairs={{0,24},{4,28},{8,16},{12,20},{16,8},{20,12},{24,0},{28,4},{1,25},{... | collective-permute-start | bytes 393224 | tf_op jit(solution)/shard_map/ppermute | solution.py:20
  36.6 3.6 %collective-permute-start.8 = (bf16[256,256]{1,0:T(8,128)(2,1)S(1)}, bf16[256,256]{1,0:T(8,128)(2,1)S(1)}, u32[]{:S(2)}, u32[]{:S(2)}) collective-permute-start(bf16[256,256]{1,0:T(8,128)(2,1)S(1)} %get-tuple-element.41), channel_id=1, source_target_pairs={{0,16},{4,20},{8,24},{12,28},{16,0},{20,4},{24,8},{28,12},{1,17},{... | collective-permute-start | bytes 393224 | tf_op jit(solution)/shard_map/ppermute | solution.py:20
  45.4 5.4 %collective-permute-done.4 = s32[512]{0:T(512)} collective-permute-done((s32[512]{0:T(512)}, s32[512]{0:T(512)}, u32[]{:S(2)}, u32[]{:S(2)}) %collective-permute-start.4) | collective-permute-done | bytes 2080 | tf_op jit(solution)/shard_map/ppermute | solution.py:20
  52.2 11.6 %collective-permute-done.5 = s32[512]{0:T(512)} collective-permute-done((s32[512]{0:T(512)}, s32[512]{0:T(512)}, u32[]{:S(2)}, u32[]{:S(2)}) %collective-permute-start.5) | collective-permute-done | bytes 2080 | tf_op jit(solution)/shard_map/ppermute | solution.py:20
  72.3 6.8 %assemble.1 = (bf16[1024,1024]{1,0:T(8,128)(2,1)}, bf16[1024,1024]{1,0:T(8,128)(2,1)}) custom-call(s32[2048]{0:T(1024)} %concatenate.25.code_ref, s32[3]{0:T(128)} %pad_add_fusion.1.place_ref, bf16[64,128,128]{2,1,0:T(8,128)(2,1)} %copy-done), custom_call_target="tpu_custom_call" | custom-call | tf_op jit(solution)/shard_map/assemble/pallas_call | solution.py:78
  80.5 3.0 %collective-permute-done.14 = bf16[1024,1024]{1,0:T(8,128)(2,1)S(1)} collective-permute-done((bf16[1024,1024]{1,0:T(8,128)(2,1)}, bf16[1024,1024]{1,0:T(8,128)(2,1)S(1)}, u32[]{:S(2)}, u32[]{:S(2)}) %collective-permute-start.14) | collective-permute-done | bytes 2097184 | tf_op jit(solution)/shard_map/ppermute | solution.py:20
  83.4 2.1 fusion.59
  90.7 3.4 %project_part.2 = f32[256,256]{1,0:T(8,128)} custom-call(bf16[1024,256]{1,0:T(8,128)(2,1)} %copy-done.4, bf16[1024,256]{1,0:T(8,128)(2,1)} %collective-permute-done.13.refs_1_, f32[1024,256]{1,0:T(8,128)} %fusion.60.refs_2_, f32[1024,256]{1,0:T(8,128)} %fusion.61.refs_3_, f32[256,256]{1,0:T(8,128)} %fusion.21.refs_4_), custom_call_target="tpu_custom_call" | custom-call | tf_op jit(solution)/shard_map/project_part/pallas_call | solution.py:106
  94.2 9.6 %all-to-all-start.1 = ((f32[32,8,256]{2,1,0:T(8,128)}), f32[32,8,256]{2,1,0:T(8,128)S(1)}, u32[]{:S(2)}, u32[]{:S(2)}) async-start(f32[32,8,256]{2,1,0:T(8,128)} %bitcast.58), calls=%async_computation.1 | async-start | bytes 524288 | tf_op jit(solution)/shard_map/all_to_all | solution.py:32
  104.0 8.5 %all-to-all-done.1 = f32[32,8,256]{2,1,0:T(8,128)S(1)} async-done(((f32[32,8,256]{2,1,0:T(8,128)}), f32[32,8,256]{2,1,0:T(8,128)S(1)}, u32[]{:S(2)}, u32[]{:S(2)}) %all-to-all-start.1) | async-done | bytes 262176 | tf_op jit(solution)/shard_map/all_to_all | solution.py:32
  113.3 4.7 %all-to-all-start.2 = ((f32[32,8,256]{2,1,0:T(8,128)}), f32[32,8,256]{2,1,0:T(8,128)S(1)}, u32[]{:S(2)}, u32[]{:S(2)}) async-start(f32[32,8,256]{2,1,0:T(8,128)} %broadcast_in_dim.8), calls=%async_computation.2 | async-start | bytes 524288 | tf_op jit(solution)/shard_map/all_to_all | solution.py:26
  118.0 2.0 fusion.58
  124.0 14.0 %all-to-all-done.2 = f32[32,8,256]{2,1,0:T(8,128)S(1)} async-done(((f32[32,8,256]{2,1,0:T(8,128)}), f32[32,8,256]{2,1,0:T(8,128)S(1)}, u32[]{:S(2)}, u32[]{:S(2)}) %all-to-all-start.2) | async-done | bytes 262176 | tf_op jit(solution)/shard_map/all_to_all | solution.py:26
  141.0 2.6 collective-permute-start.20
  144.2 2.6 collective-permute-done.16
  150.0 4.2 %collective-permute-done.20 = f32[256,256]{1,0:T(8,128)S(1)} collective-permute-done((f32[256,256]{1,0:T(8,128)S(1)}, f32[256,256]{1,0:T(8,128)S(1)}, u32[]{:S(2)}, u32[]{:S(2)}) %collective-permute-start.20) | collective-permute-done | bytes 262176 | tf_op jit(solution)/shard_map/ppermute | solution.py:20
  154.5 9.2 %all_to_all.35 = f32[32,2,256]{2,1,0:T(2,128)S(1)} all-to-all(f32[32,2,256]{2,1,0:T(2,128)S(1)} %broadcast_in_dim.9), channel_id=1, replica_groups=mesh['row'=8,'col'=4] {'row','col'}, dimensions={0} | all-to-all | bytes 131072 | tf_op jit(solution)/shard_map/all_to_all | solution.py:26
  167.4 3.8 %collective-permute-done.24 = bf16[256,256]{1,0:T(8,128)(2,1)S(1)} collective-permute-done((bf16[256,256]{1,0:T(8,128)(2,1)S(1)}, bf16[256,256]{1,0:T(8,128)(2,1)S(1)}, u32[]{:S(2)}, u32[]{:S(2)}) %collective-permute-start.24) | collective-permute-done | bytes 131104 | tf_op jit(solution)/shard_map/ppermute | solution.py:20
  174.0 3.2 %collective-permute-start.27 = (bf16[256,256]{1,0:T(8,128)(2,1)S(1)}, bf16[256,256]{1,0:T(8,128)(2,1)S(1)}, u32[]{:S(2)}, u32[]{:S(2)}) collective-permute-start(bf16[256,256]{1,0:T(8,128)(2,1)S(1)} %fusion.53), channel_id=1, source_target_pairs={{0,16},{4,20},{8,24},{12,28},{16,0},{20,4},{24,8},{28,12},{1,17},{... | collective-permute-start | bytes 393224 | tf_op jit(solution)/shard_map/ppermute | solution.py:20
  178.5 6.8 %collective-permute-done.28 = bf16[256,256]{1,0:T(8,128)(2,1)S(1)} collective-permute-done((bf16[256,256]{1,0:T(8,128)(2,1)S(1)}, bf16[256,256]{1,0:T(8,128)(2,1)S(1)}, u32[]{:S(2)}, u32[]{:S(2)}) %collective-permute-start.28) | collective-permute-done | bytes 131104 | tf_op jit(solution)/shard_map/ppermute | solution.py:20
  191.9 3.3 %project_part.3 = f32[256,256]{1,0:T(8,128)} custom-call(bf16[1024,256]{1,0:T(8,128)(2,1)} %copy-done.5, bf16[1024,256]{1,0:T(8,128)(2,1)} %copy-done.9, f32[1024,256]{1,0:T(8,128)} %fusion.63.refs_2_, f32[1024,256]{1,0:T(8,128)} %copy-done.7, f32[256,256]{1,0:T(8,128)} %fusion.19.refs_4_), custom_call_target="tpu_custom_call" | custom-call | tf_op jit(solution)/shard_map/project_part/pallas_call | solution.py:106
  195.3 14.8 %all_to_all.36 = f32[32,8,256]{2,1,0:T(8,128)S(1)} all-to-all(f32[32,8,256]{2,1,0:T(8,128)} %bitcast.59), channel_id=1, replica_groups=mesh['row'=8,'col'=4] {'row','col'}, dimensions={0} | all-to-all | bytes 524288 | tf_op jit(solution)/shard_map/all_to_all | solution.py:32
  210.9 4.7 %all-to-all-start.5 = ((f32[32,8,256]{2,1,0:T(8,128)}), f32[32,8,256]{2,1,0:T(8,128)S(1)}, u32[]{:S(2)}, u32[]{:S(2)}) async-start(f32[32,8,256]{2,1,0:T(8,128)} %broadcast_in_dim.10), calls=%async_computation.5 | async-start | bytes 524288 | tf_op jit(solution)/shard_map/all_to_all | solution.py:26
  225.0 16.2 %collective-permute-done.35 = f32[256,256]{1,0:T(8,128)S(1)} collective-permute-done((f32[256,256]{1,0:T(8,128)S(1)}, f32[256,256]{1,0:T(8,128)S(1)}, u32[]{:S(2)}, u32[]{:S(2)}) %collective-permute-start.35) | collective-permute-done | bytes 262176 | tf_op jit(solution)/shard_map/ppermute | solution.py:20
  241.8 2.5 collective-permute-done.34
  246.5 2.0 collective-permute-done.30
  250.7 4.8 %all-to-all-start.6 = ((f32[32,2,256]{2,1,0:T(2,128)}), f32[32,2,256]{2,1,0:T(2,128)S(1)}, u32[]{:S(2)}, u32[]{:S(2)}) async-start(f32[32,2,256]{2,1,0:T(2,128)} %broadcast_in_dim.11), calls=%async_computation.6 | async-start | bytes 131072 | tf_op jit(solution)/shard_map/all_to_all | solution.py:26
  256.4 4.4 %all-to-all-done.6 = f32[32,2,256]{2,1,0:T(2,128)S(1)} async-done(((f32[32,2,256]{2,1,0:T(2,128)}), f32[32,2,256]{2,1,0:T(2,128)S(1)}, u32[]{:S(2)}, u32[]{:S(2)}) %all-to-all-start.6) | async-done | bytes 65568 | tf_op jit(solution)/shard_map/all_to_all | solution.py:26
  (147 shorter events, 69.6 us)
Async XLA Ops:
  0.7 70.2 %all-to-all-start = ((bf16[64,128,128]{2,1,0:T(8,128)(2,1)}), bf16[64,128,128]{2,1,0:T(8,128)(2,1)S(1)}, u32[]{:S(2)}, u32[]{:S(2)}) async-start(bf16[64,128,128]{2,1,0:T(8,128)(2,1)} %param.6), calls=%async_computation | async-start | bytes 4194304 | tf_op jit(solution)/shard_map/all_to_all | solution.py:140
  6.9 19.3 %collective-permute-start.12 = (bf16[256,256]{1,0:T(8,128)(2,1)S(1)}, bf16[256,256]{1,0:T(8,128)(2,1)S(1)}, u32[]{:S(2)}, u32[]{:S(2)}) collective-permute-start(bf16[256,256]{1,0:T(8,128)(2,1)S(1)} %get-tuple-element.27), channel_id=1, source_target_pairs={{0,3},{1,2},{2,1},{3,0},{4,7},{5,6},{6,5},{7,4},{8,11},{9,10},{10,... | collective-permute-start | bytes 393224 | tf_op jit(solution)/shard_map/ppermute | solution.py:20
  8.4 21.4 %collective-permute-start.11 = (bf16[256,256]{1,0:T(8,128)(2,1)S(1)}, bf16[256,256]{1,0:T(8,128)(2,1)S(1)}, u32[]{:S(2)}, u32[]{:S(2)}) collective-permute-start(bf16[256,256]{1,0:T(8,128)(2,1)S(1)} %get-tuple-element.27), channel_id=1, source_target_pairs={{0,2},{1,3},{2,0},{3,1},{4,6},{5,7},{6,4},{7,5},{8,10},{9,11},{10,... | collective-permute-start | bytes 393224 | tf_op jit(solution)/shard_map/ppermute | solution.py:20
  8.9 20.9 %collective-permute-start.10 = (bf16[256,256]{1,0:T(8,128)(2,1)S(1)}, bf16[256,256]{1,0:T(8,128)(2,1)S(1)}, u32[]{:S(2)}, u32[]{:S(2)}) collective-permute-start(bf16[256,256]{1,0:T(8,128)(2,1)S(1)} %get-tuple-element.27), channel_id=1, source_target_pairs={{0,1},{1,0},{2,3},{3,2},{4,5},{5,4},{6,7},{7,6},{8,9},{9,8},{10,11... | collective-permute-start | bytes 393224 | tf_op jit(solution)/shard_map/ppermute | solution.py:20
  29.9 41.0 %collective-permute-start.13 = (bf16[1024,256]{1,0:T(8,128)(2,1)S(1)}, bf16[1024,256]{1,0:T(8,128)(2,1)}, u32[]{:S(2)}, u32[]{:S(2)}) collective-permute-start(bf16[1024,256]{1,0:T(8,128)(2,1)S(1)} %pad_maximum_fusion.1.refs_0_), channel_id=1, source_target_pairs={{0,4},{4,0},{8,12},{12,8},{16,20},{20,16},{24,28},{28,24},{1,5},{5... | collective-permute-start | bytes 1572872 | tf_op jit(solution)/shard_map/ppermute | solution.py:20
  31.0 9.2 %collective-permute-start.1 = (s32[64]{0:T(128)S(1)}, s32[64]{0:T(128)S(1)}, u32[]{:S(2)}, u32[]{:S(2)}) collective-permute-start(s32[64]{0:T(128)S(1)} %copy-done.14), channel_id=1, source_target_pairs={{0,2},{1,3},{2,0},{3,1},{4,6},{5,7},{6,4},{7,5},{8,10},{9,11},{10,... | collective-permute-start | bytes 776 | tf_op jit(solution)/shard_map/ppermute | solution.py:20
  31.0 10.8 %collective-permute-start.2 = (s32[64]{0:T(128)S(1)}, s32[64]{0:T(128)S(1)}, u32[]{:S(2)}, u32[]{:S(2)}) collective-permute-start(s32[64]{0:T(128)S(1)} %copy-done.14), channel_id=1, source_target_pairs={{0,3},{1,2},{2,1},{3,0},{4,7},{5,6},{6,5},{7,4},{8,11},{9,10},{10,... | collective-permute-start | bytes 776 | tf_op jit(solution)/shard_map/ppermute | solution.py:20
  33.5 35.6 %collective-permute-start.9 = (bf16[256,256]{1,0:T(8,128)(2,1)S(1)}, bf16[256,256]{1,0:T(8,128)(2,1)S(1)}, u32[]{:S(2)}, u32[]{:S(2)}) collective-permute-start(bf16[256,256]{1,0:T(8,128)(2,1)S(1)} %get-tuple-element.41), channel_id=1, source_target_pairs={{0,24},{4,28},{8,16},{12,20},{16,8},{20,12},{24,0},{28,4},{1,25},{... | collective-permute-start | bytes 393224 | tf_op jit(solution)/shard_map/ppermute | solution.py:20
  36.6 32.6 %collective-permute-start.8 = (bf16[256,256]{1,0:T(8,128)(2,1)S(1)}, bf16[256,256]{1,0:T(8,128)(2,1)S(1)}, u32[]{:S(2)}, u32[]{:S(2)}) collective-permute-start(bf16[256,256]{1,0:T(8,128)(2,1)S(1)} %get-tuple-element.41), channel_id=1, source_target_pairs={{0,16},{4,20},{8,24},{12,28},{16,0},{20,4},{24,8},{28,12},{1,17},{... | collective-permute-start | bytes 393224 | tf_op jit(solution)/shard_map/ppermute | solution.py:20
  40.2 29.0 %collective-permute-start.7 = (bf16[256,256]{1,0:T(8,128)(2,1)S(1)}, bf16[256,256]{1,0:T(8,128)(2,1)}, u32[]{:S(2)}, u32[]{:S(2)}) collective-permute-start(bf16[256,256]{1,0:T(8,128)(2,1)S(1)} %get-tuple-element.41), channel_id=1, source_target_pairs={{0,8},{4,12},{8,0},{12,4},{16,24},{20,28},{24,16},{28,20},{1,9},{5... | collective-permute-start | bytes 393224 | tf_op jit(solution)/shard_map/ppermute | solution.py:20
  50.8 13.0 %collective-permute-start.5 = (s32[512]{0:T(512)}, s32[512]{0:T(512)}, u32[]{:S(2)}, u32[]{:S(2)}) collective-permute-start(s32[512]{0:T(512)} %concatenate.24), channel_id=1, source_target_pairs={{0,16},{4,20},{8,24},{12,28},{16,0},{20,4},{24,8},{28,12},{1,17},{... | collective-permute-start | bytes 6152 | tf_op jit(solution)/shard_map/ppermute | solution.py:20
  94.2 18.4 %all-to-all-start.1 = ((f32[32,8,256]{2,1,0:T(8,128)}), f32[32,8,256]{2,1,0:T(8,128)S(1)}, u32[]{:S(2)}, u32[]{:S(2)}) async-start(f32[32,8,256]{2,1,0:T(8,128)} %bitcast.58), calls=%async_computation.1 | async-start | bytes 524288 | tf_op jit(solution)/shard_map/all_to_all | solution.py:32
  103.8 34.6 %collective-permute-start.18 = (f32[1024,256]{1,0:T(8,128)S(1)}, f32[1024,256]{1,0:T(8,128)}, u32[]{:S(2)}, u32[]{:S(2)}) collective-permute-start(f32[1024,256]{1,0:T(8,128)S(1)} %copy-done.6), channel_id=1, source_target_pairs={{0,4},{4,0},{8,12},{12,8},{16,20},{20,16},{24,28},{28,24},{1,5},{5... | collective-permute-start | bytes 3145736 | tf_op jit(solution)/shard_map/ppermute | solution.py:20
  113.3 24.7 %all-to-all-start.2 = ((f32[32,8,256]{2,1,0:T(8,128)}), f32[32,8,256]{2,1,0:T(8,128)S(1)}, u32[]{:S(2)}, u32[]{:S(2)}) async-start(f32[32,8,256]{2,1,0:T(8,128)} %broadcast_in_dim.8), calls=%async_computation.2 | async-start | bytes 524288 | tf_op jit(solution)/shard_map/all_to_all | solution.py:26
  120.0 23.6 %collective-permute-start.17 = (f32[256,256]{1,0:T(8,128)}, f32[256,256]{1,0:T(8,128)S(1)}, u32[]{:S(2)}, u32[]{:S(2)}) collective-permute-start(f32[256,256]{1,0:T(8,128)} %get-tuple-element.39), channel_id=1, source_target_pairs={{0,24},{4,28},{8,16},{12,20},{16,8},{20,12},{24,0},{28,4},{1,25},{... | collective-permute-start | bytes 786440 | tf_op jit(solution)/shard_map/ppermute | solution.py:20
  121.6 25.2 %collective-permute-start.16 = (f32[256,256]{1,0:T(8,128)}, f32[256,256]{1,0:T(8,128)S(1)}, u32[]{:S(2)}, u32[]{:S(2)}) collective-permute-start(f32[256,256]{1,0:T(8,128)} %get-tuple-element.40), channel_id=1, source_target_pairs={{0,16},{4,20},{8,24},{12,28},{16,0},{20,4},{24,8},{28,12},{1,17},{... | collective-permute-start | bytes 786440 | tf_op jit(solution)/shard_map/ppermute | solution.py:20
  122.9 23.8 %collective-permute-start.15 = (f32[256,256]{1,0:T(8,128)}, f32[256,256]{1,0:T(8,128)}, u32[]{:S(2)}, u32[]{:S(2)}) collective-permute-start(f32[256,256]{1,0:T(8,128)} %get-tuple-element.38), channel_id=1, source_target_pairs={{0,8},{4,12},{8,0},{12,4},{16,24},{20,28},{24,16},{28,20},{1,9},{5... | collective-permute-start | bytes 786440 | tf_op jit(solution)/shard_map/ppermute | solution.py:20
  139.8 10.2 %collective-permute-start.21 = (f32[256,256]{1,0:T(8,128)S(1)}, f32[256,256]{1,0:T(8,128)S(1)}, u32[]{:S(2)}, u32[]{:S(2)}) collective-permute-start(f32[256,256]{1,0:T(8,128)S(1)} %get-tuple-element.36), channel_id=1, source_target_pairs={{0,3},{1,2},{2,1},{3,0},{4,7},{5,6},{6,5},{7,4},{8,11},{9,10},{10,... | collective-permute-start | bytes 786440 | tf_op jit(solution)/shard_map/ppermute | solution.py:20
  141.0 13.2 %collective-permute-start.20 = (f32[256,256]{1,0:T(8,128)S(1)}, f32[256,256]{1,0:T(8,128)S(1)}, u32[]{:S(2)}, u32[]{:S(2)}) collective-permute-start(f32[256,256]{1,0:T(8,128)S(1)} %get-tuple-element.37), channel_id=1, source_target_pairs={{0,2},{1,3},{2,0},{3,1},{4,6},{5,7},{6,4},{7,5},{8,10},{9,11},{10,... | collective-permute-start | bytes 786440 | tf_op jit(solution)/shard_map/ppermute | solution.py:20
  143.6 10.6 %collective-permute-start.19 = (f32[256,256]{1,0:T(8,128)S(1)}, f32[256,256]{1,0:T(8,128)S(1)}, u32[]{:S(2)}, u32[]{:S(2)}) collective-permute-start(f32[256,256]{1,0:T(8,128)S(1)} %get-tuple-element.35), channel_id=1, source_target_pairs={{0,1},{1,0},{2,3},{3,2},{4,5},{5,4},{6,7},{7,6},{8,9},{9,8},{10,11... | collective-permute-start | bytes 786440 | tf_op jit(solution)/shard_map/ppermute | solution.py:20
  173.2 12.7 %collective-permute-start.25 = (bf16[1024,256]{1,0:T(8,128)(2,1)S(1)}, bf16[1024,256]{1,0:T(8,128)(2,1)S(1)}, u32[]{:S(2)}, u32[]{:S(2)}) collective-permute-start(bf16[1024,256]{1,0:T(8,128)(2,1)S(1)} %pad_maximum_fusion.2.refs_0_), channel_id=1, source_target_pairs={{0,4},{4,0},{8,12},{12,8},{16,20},{20,16},{24,28},{28,24},{1,5},{5... | collective-permute-start | bytes 1572872 | tf_op jit(solution)/shard_map/ppermute | solution.py:20
  173.3 12.1 %collective-permute-start.28 = (bf16[256,256]{1,0:T(8,128)(2,1)S(1)}, bf16[256,256]{1,0:T(8,128)(2,1)S(1)}, u32[]{:S(2)}, u32[]{:S(2)}) collective-permute-start(bf16[256,256]{1,0:T(8,128)(2,1)S(1)} %fusion.53), channel_id=1, source_target_pairs={{0,24},{4,28},{8,16},{12,20},{16,8},{20,12},{24,0},{28,4},{1,25},{... | collective-permute-start | bytes 393224 | tf_op jit(solution)/shard_map/ppermute | solution.py:20
  174.0 11.8 %collective-permute-start.27 = (bf16[256,256]{1,0:T(8,128)(2,1)S(1)}, bf16[256,256]{1,0:T(8,128)(2,1)S(1)}, u32[]{:S(2)}, u32[]{:S(2)}) collective-permute-start(bf16[256,256]{1,0:T(8,128)(2,1)S(1)} %fusion.53), channel_id=1, source_target_pairs={{0,16},{4,20},{8,24},{12,28},{16,0},{20,4},{24,8},{28,12},{1,17},{... | collective-permute-start | bytes 393224 | tf_op jit(solution)/shard_map/ppermute | solution.py:20
  177.2 8.7 %collective-permute-start.26 = (bf16[256,256]{1,0:T(8,128)(2,1)S(1)}, bf16[256,256]{1,0:T(8,128)(2,1)S(1)}, u32[]{:S(2)}, u32[]{:S(2)}) collective-permute-start(bf16[256,256]{1,0:T(8,128)(2,1)S(1)} %fusion.53), channel_id=1, source_target_pairs={{0,8},{4,12},{8,0},{12,4},{16,24},{20,28},{24,16},{28,20},{1,9},{5... | collective-permute-start | bytes 393224 | tf_op jit(solution)/shard_map/ppermute | solution.py:20
  190.2 31.4 %collective-permute-start.29 = (f32[1024,256]{1,0:T(8,128)S(1)}, f32[1024,256]{1,0:T(8,128)}, u32[]{:S(2)}, u32[]{:S(2)}) collective-permute-start(f32[1024,256]{1,0:T(8,128)S(1)} %fusion.64.refs_3_), channel_id=1, source_target_pairs={{0,4},{4,0},{8,12},{12,8},{16,20},{20,16},{24,28},{28,24},{1,5},{5... | collective-permute-start | bytes 3145736 | tf_op jit(solution)/shard_map/ppermute | solution.py:20
  210.9 34.1 %all-to-all-start.5 = ((f32[32,8,256]{2,1,0:T(8,128)}), f32[32,8,256]{2,1,0:T(8,128)S(1)}, u32[]{:S(2)}, u32[]{:S(2)}) async-start(f32[32,8,256]{2,1,0:T(8,128)} %broadcast_in_dim.10), calls=%async_computation.5 | async-start | bytes 524288 | tf_op jit(solution)/shard_map/all_to_all | solution.py:26
  216.8 24.5 %collective-permute-start.35 = (f32[256,256]{1,0:T(8,128)S(1)}, f32[256,256]{1,0:T(8,128)S(1)}, u32[]{:S(2)}, u32[]{:S(2)}) collective-permute-start(f32[256,256]{1,0:T(8,128)S(1)} %get-tuple-element.30), channel_id=1, source_target_pairs={{0,24},{4,28},{8,16},{12,20},{16,8},{20,12},{24,0},{28,4},{1,25},{... | collective-permute-start | bytes 786440 | tf_op jit(solution)/shard_map/ppermute | solution.py:20
  218.4 25.9 %collective-permute-start.34 = (f32[256,256]{1,0:T(8,128)S(1)}, f32[256,256]{1,0:T(8,128)S(1)}, u32[]{:S(2)}, u32[]{:S(2)}) collective-permute-start(f32[256,256]{1,0:T(8,128)S(1)} %get-tuple-element.31), channel_id=1, source_target_pairs={{0,16},{4,20},{8,24},{12,28},{16,0},{20,4},{24,8},{28,12},{1,17},{... | collective-permute-start | bytes 786440 | tf_op jit(solution)/shard_map/ppermute | solution.py:20
  219.7 25.3 %collective-permute-start.33 = (f32[256,256]{1,0:T(8,128)S(1)}, f32[256,256]{1,0:T(8,128)}, u32[]{:S(2)}, u32[]{:S(2)}) collective-permute-start(f32[256,256]{1,0:T(8,128)S(1)} %get-tuple-element.29), channel_id=1, source_target_pairs={{0,8},{4,12},{8,0},{12,4},{16,24},{20,28},{24,16},{28,20},{1,9},{5... | collective-permute-start | bytes 786440 | tf_op jit(solution)/shard_map/ppermute | solution.py:20
  223.0 23.6 %collective-permute-start.32 = (f32[256,256]{1,0:T(8,128)S(1)}, f32[256,256]{1,0:T(8,128)}, u32[]{:S(2)}, u32[]{:S(2)}) collective-permute-start(f32[256,256]{1,0:T(8,128)S(1)} %get-tuple-element.33), channel_id=1, source_target_pairs={{0,3},{1,2},{2,1},{3,0},{4,7},{5,6},{6,5},{7,4},{8,11},{9,10},{10,... | collective-permute-start | bytes 786440 | tf_op jit(solution)/shard_map/ppermute | solution.py:20
  224.5 22.0 %collective-permute-start.31 = (f32[256,256]{1,0:T(8,128)S(1)}, f32[256,256]{1,0:T(8,128)}, u32[]{:S(2)}, u32[]{:S(2)}) collective-permute-start(f32[256,256]{1,0:T(8,128)S(1)} %get-tuple-element.34), channel_id=1, source_target_pairs={{0,2},{1,3},{2,0},{3,1},{4,6},{5,7},{6,4},{7,5},{8,10},{9,11},{10,... | collective-permute-start | bytes 786440 | tf_op jit(solution)/shard_map/ppermute | solution.py:20
  250.7 10.1 %all-to-all-start.6 = ((f32[32,2,256]{2,1,0:T(2,128)}), f32[32,2,256]{2,1,0:T(2,128)S(1)}, u32[]{:S(2)}, u32[]{:S(2)}) async-start(f32[32,2,256]{2,1,0:T(2,128)} %broadcast_in_dim.11), calls=%async_computation.6 | async-start | bytes 131072 | tf_op jit(solution)/shard_map/all_to_all | solution.py:26
  (31 other events, 369.3 us)

commit v3 on v2

--- a/solution.py
+++ b/solution.py
@@ -10,9 +10,16 @@
 AXES = ("row", "col")
 
 epsilon = 1e-06
+VMEM_BYTES = 4 * 2**20
 bf16 = jnp.bfloat16
 f32 = jnp.float32
 FIRST = (((0,), (0,)), ((), ()))
+
+
+def in_vmem(*arrays):
+    if sum(array.size * array.dtype.itemsize for array in arrays) > VMEM_BYTES:
+        return arrays
+    return tuple(pltpu.with_memory_space_constraint(array, pltpu.VMEM) for array in arrays)
 
 
 def partner(value, axis, offset):
@@ -34,46 +41,54 @@
     return copies_of_all(piece).reshape(whole.shape)
 
 
+def bits_of(size):
+    return size.bit_length() - 1
+
+
+def reverse_bits(value, count):
+    return sum(((value >> bit) & 1) << (count - 1 - bit) for bit in range(count))
+
+
 def assemble(tiles, codes, place, levels, col_size):
     slots, tile, _ = tiles.shape
-    grid_cols = 4 * levels
     cap = slots // (2 * levels * col_size)
+    grid_bits = bits_of(4 * levels)
     shape = jax.ShapeDtypeStruct((2 * col_size * tile, 2 * levels * tile), tiles.dtype)
 
     def kernel(code_ref, place_ref, tile_ref, own_ref, sib_ref):
         level, core, col = place_ref[0], place_ref[1], place_ref[2]
-        me = (level * 2 + core) * col_size + col
+        mine = ((level * 2 + core) * col_size + col) * cap
         own_ref[...] = jnp.zeros_like(own_ref)
         sib_ref[...] = jnp.zeros_like(sib_ref)
 
         def put(slot, carry):
-            source = slot // cap
-            source_row = source // col_size
-            near = ((source_row // 2) ^ level) * 2 + ((source_row % 2) ^ core)
-            near = near * col_size + ((source % col_size) ^ col)
-            code = code_ref[near * slots + me * cap + slot % cap]
+            source = slot >> bits_of(cap)
+            source_row = source >> bits_of(col_size)
+            near = ((source_row >> 1) ^ level) * 2 + ((source_row & 1) ^ core)
+            near = near * col_size + ((source & (col_size - 1)) ^ col)
+            code = code_ref[near * slots + mine + (slot & (cap - 1))]
 
             @pl.when(code >= 0)
             def _():
-                block_row = code // grid_cols
-                block_col = code % grid_cols
-                owner_row = block_col // 2
-                down = ((block_row // 2) ^ col) * 2 + block_row % 2
-                across = ((owner_row // 2) ^ level) * 2 + block_col % 2
+                block_row = code >> grid_bits
+                block_col = code & ((1 << grid_bits) - 1)
+                owner_row = block_col >> 1
+                down = ((block_row >> 1) ^ col) * 2 + (block_row & 1)
+                across = reverse_bits((owner_row >> 1) ^ level, bits_of(levels)) * 2 + (block_col & 1)
                 rows = pl.ds(pl.multiple_of(down * tile, tile), tile)
                 cols = pl.ds(pl.multiple_of(across * tile, tile), tile)
 
-                @pl.when(owner_row % 2 == core)
+                @pl.when((owner_row & 1) == core)
                 def _():
                     own_ref[rows, cols] = tile_ref[slot]
 
-                @pl.when(owner_row % 2 != core)
+                @pl.when((owner_row & 1) != core)
                 def _():
                     sib_ref[rows, cols] = tile_ref[slot]
 
             return carry
 
-        lax.fori_loop(0, slots, put, 0)
+        lax.fori_loop(0, slots, put, 0, unroll=4)
 
     return pl.pallas_call(
         kernel,
@@ -87,8 +102,8 @@
     )(codes, place, tiles)
 
 
-def project_part(left, right, extra):
-    rows, ports = left[0].shape
+def project_part(left_own, left_sib, right_own, right_sib, extra):
+    rows, ports = left_own.shape
 
     def kernel(*refs):
         lefts, rights, extra_ref, out_ref = refs[:2], refs[2:4], refs[4], refs[5]
@@ -105,7 +120,7 @@
 
     return pl.pallas_call(
         kernel, out_shape=jax.ShapeDtypeStruct((ports, ports), f32), name="project_part"
-    )(*left, *right, extra)
+    )(left_own, left_sib, right_own, right_sib, extra)
 
 
 def local(tile_values, slot_codes, right_start, left_start, node_diagonal, row_scale):
@@ -118,9 +133,8 @@
     place = jnp.stack([row_index // 2, row_index % 2, lax.axis_index("col")]).astype(jnp.int32)
 
     def gather(right, left):
-        right_all = jnp.concatenate(
-            [right] + [partner(right, "row", 2 * k) for k in range(1, levels)], axis=0
-        )
+        order = [reverse_bits(k, bits_of(levels)) for k in range(levels)]
+        right_all = [right] + [partner(right, "row", 2 * k) for k in order[1:]]
         left_own = jnp.concatenate([left] + [partner(left, "col", k) for k in range(1, col_size)], axis=0)
         return right_all, left_own, partner(left_own, "row", 1)
 
@@ -134,32 +148,49 @@
         scaled_left = scale_col * left_vec
         left_bf = scaled_left.astype(bf16)
         diag_right = diag_col * right_vec
+        right_all, left_own, left_sib = gather(right_bf, left_bf)
         local_proj = lax.dot_general(scaled_left, diag_right, FIRST, precision=lax.Precision.HIGHEST)
-        right_all, left_own, left_sib = gather(right_bf, left_bf)
         if turn == 0:
             got_tiles = lax.all_to_all(tile_values, AXES, split_axis=0, concat_axis=0, tiled=True)
             codes = slot_codes
-            for axis, offsets in (
-                ("col", range(1, col_size)),
-                ("row", (1,)),
-                ("row", range(2, row_size, 2)),
-            ):
+            for axis, offsets in (("col", range(1, col_size)), ("row", (1,)), ("row", range(2, row_size, 2))):
                 codes = jnp.concatenate([codes] + [partner(codes, axis, k) for k in offsets])
-            got_tiles, codes, right_all, left_own, left_sib = lax.optimization_barrier(
-                (got_tiles, codes, right_all, left_own, left_sib)
+            got_tiles, codes, left_own, left_sib, local_proj = lax.optimization_barrier(
+                (got_tiles, codes, left_own, left_sib, local_proj)
             )
+            (got_tiles,) = in_vmem(got_tiles)
             own_half, sib_half = assemble(got_tiles, codes, place, levels, col_size)
             other_half = partner(sib_half, "row", 1)
-        left_part = lax.dot_general(own_half, left_own, FIRST, preferred_element_type=f32) + lax.dot_general(
-            other_half, left_sib, FIRST, preferred_element_type=f32
-        )
-        left_part, right_all = lax.optimization_barrier((left_part, right_all))
+        else:
+            right_all, left_own, left_sib, local_proj = lax.optimization_barrier(
+                (right_all, left_own, left_sib, local_proj)
+            )
+        right_all = jnp.concatenate(right_all, axis=0)
+        half = levels * rows // 2
+
+        def left_dots(cols):
+            return lax.dot_general(
+                own_half[:, cols], left_own, FIRST, preferred_element_type=f32
+            ) + lax.dot_general(other_half[:, cols], left_sib, FIRST, preferred_element_type=f32)
+
+        left_send = left_dots(slice(half, None))
+        left_keep = left_dots(slice(0, half))
+        if turn == 0:
+            left_send, right_last = lax.optimization_barrier((left_send, right_all))
+        else:
+            left_send, right_all = lax.optimization_barrier((left_send, right_all))
+            right_last = right_all
         right_own = jnp.dot(own_half, right_all, preferred_element_type=f32)
-        right_sib = jnp.dot(other_half, right_all, preferred_element_type=f32)
-        left_prod = left_part[:rows]
-        for k in range(1, levels):
-            left_prod += partner(left_part[k * rows : (k + 1) * rows], "row", 2 * k)
-        project = project_part((left_own, left_sib), (right_own, right_sib), local_proj)
+        right_sib = jnp.dot(other_half, right_last, preferred_element_type=f32)
+        for bit in range(bits_of(levels)):
+            left_got = partner(left_send, "row", 2 << bit)
+            kept = left_keep.shape[0] // 2
+            if kept >= rows:
+                left_send = left_keep[kept:] + left_got[kept:]
+                left_keep = left_keep[:kept] + left_got[:kept]
+            else:
+                left_prod = left_keep + left_got
+        project = project_part(*in_vmem(left_own, left_sib, right_own, right_sib, local_proj))
         project = sum_over_all(project) / order_rows
         right_got = partner(right_sib, "row", 1)
         right_pair = right_own + right_got

time: 266 us -> 228 us (0.86)
  waiting for transfers between devices: 112 us -> 92.8 us
  blocking collectives: 24.1 us -> 8.72 us
  local copies, waits for them, and re-layouts: 11.8 us -> 7.12 us
  Pallas kernels: 13.5 us -> 9.68 us
    all_to_all x1 -> x0, blocking collectives: 14.8 us -> none  [sum_over_all(): lax.all_to_all(pieces, AXES, split_axis=0, concat_axis=0, tiled=True)]
    all_to_all x3, waiting for transfers between devices: 18.4 us -> 4.45 us  [copies_of_all(): return lax.all_to_all(copies, AXES, split_axis=0, concat_axis=0, tiled=True)]
    ppermute x36 -> x34, waiting for transfers between devices: 85 us -> 76.7 us  [partner(): lax.ppermute(value, axis, [(index, index ^ offset) for index in range(siz...]
    dot_general x6 -> x10, matrix products: 8.78 us -> 13.9 us  [the longest x4 5.75 us: left_dots(): lax.dot_general(other_half[:, cols], left_sib, FIRST, preferred_element_t...]
    slice x2 -> x0, local copies, waits for them, and re-layouts: 3.2 us -> none  [local(): left_prod += partner(left_part[k * rows:(k + 1) * rows], 'row', 2 * k)]
    all_to_all x1 -> x2, waiting for transfers between devices: 8.52 us -> 11.6 us  [sum_over_all(): lax.all_to_all(pieces, AXES, split_axis=0, concat_axis=0, tiled=True)]
    all_to_all x1 -> x2, starting transfers between devices: 9.64 us -> 11.5 us  [sum_over_all(): lax.all_to_all(pieces, AXES, split_axis=0, concat_axis=0, tiled=True)]
    ppermute x36 -> x34, starting transfers between devices: 41.3 us -> 43 us  [partner(): lax.ppermute(value, axis, [(index, index ^ offset) for index in range(siz...]
  transfers between devices with their start and end apart: 41 -> 40, of which waited for: 20 -> 25; matrix products, arithmetic and copies ran while one was open for 9% -> 10% of each run, Pallas kernels for 1% -> 2%
where the time goes in v3:
time: 228 us; the launch traced here: 224 us
  waiting for transfers between devices  92.8 us (41%)
  starting transfers between devices  73.5 us (32%)
  matrix products  21.5 us (9%)
  Pallas kernels  9.68 us (4%)
  other arithmetic  9.21 us (4%)
  blocking collectives  8.72 us (4%)
  local copies, waits for them, and re-layouts  7.12 us (3%)
    ppermute x34, waiting for transfers between devices, partner(): lax.ppermute(value, axis, [(index, index ^ offset) for index in range(siz...  76.7 us
    ppermute x34, starting transfers between devices, partner(): lax.ppermute(value, axis, [(index, index ^ offset) for index in range(siz...  43 us
    all_to_all x3, starting transfers between devices, copies_of_all(): return lax.all_to_all(copies, AXES, split_axis=0, concat_axis=0, tiled=True)  13 us
    all_to_all x2, waiting for transfers between devices, sum_over_all(): lax.all_to_all(pieces, AXES, split_axis=0, concat_axis=0, tiled=True)  11.6 us
    all_to_all x2, starting transfers between devices, sum_over_all(): lax.all_to_all(pieces, AXES, split_axis=0, concat_axis=0, tiled=True)  11.5 us
    all_to_all x1, blocking collectives, copies_of_all(): return lax.all_to_all(copies, AXES, split_axis=0, concat_axis=0, tiled=True)  8.72 us
    all_to_all x1, starting transfers between devices, local(): lax.all_to_all(tile_values, AXES, split_axis=0, concat_axis=0, tiled=True)  6.02 us
    dot_general x4, matrix products, left_dots(): lax.dot_general(other_half[:, cols], left_sib, FIRST, preferred_element_t...  5.75 us
  transfers between devices with their start and end apart: 40, of which 25 were waited for; matrix products, arithmetic and copies ran while one was open for 10% of the time, Pallas kernels for 2%

profile of v3, /device:TPU:10, one launch (start us, length us, event | category | flops | bytes accessed | tf_op | source)
XLA Modules:
  0.0 223.8 jit_solution(16354797256943213683)
XLA Ops:
  0.7 6.0 %all-to-all-start = ((bf16[64,128,128]{2,1,0:T(8,128)(2,1)}), bf16[64,128,128]{2,1,0:T(8,128)(2,1)S(1)}, u32[]{:S(2)}, u32[]{:S(2)}) async-start(bf16[64,128,128]{2,1,0:T(8,128)(2,1)} %param.6), calls=%async_computation | async-start | bytes 4194304 | tf_op jit(solution)/shard_map/all_to_all | solution.py:154
  11.0 15.2 %collective-permute-done.9 = bf16[256,256]{1,0:T(8,128)(2,1)S(1)} collective-permute-done((bf16[256,256]{1,0:T(8,128)(2,1)S(1)}, bf16[256,256]{1,0:T(8,128)(2,1)S(1)}, u32[]{:S(2)}, u32[]{:S(2)}) %collective-permute-start.9) | collective-permute-done | bytes 131104 | tf_op jit(solution)/shard_map/ppermute | solution.py:27
  26.1 3.7 %collective-permute-done.8 = bf16[256,256]{1,0:T(8,128)(2,1)S(1)} collective-permute-done((bf16[256,256]{1,0:T(8,128)(2,1)S(1)}, bf16[256,256]{1,0:T(8,128)(2,1)S(1)}, u32[]{:S(2)}, u32[]{:S(2)}) %collective-permute-start.8) | collective-permute-done | bytes 131104 | tf_op jit(solution)/shard_map/ppermute | solution.py:27
  30.1 2.3 %collective-permute-start.1 = (s32[64]{0:T(128)S(1)}, s32[64]{0:T(128)S(1)}, u32[]{:S(2)}, u32[]{:S(2)}) collective-permute-start(s32[64]{0:T(128)S(1)} %copy-done.23), channel_id=1, source_target_pairs={{0,2},{1,3},{2,0},{3,1},{4,6},{5,7},{6,4},{7,5},{8,10},{9,11},{10,... | collective-permute-start | bytes 776 | tf_op jit(solution)/shard_map/ppermute | solution.py:27
  40.1 4.1 %collective-permute-start.6 = (s32[512]{0:T(512)}, s32[512]{0:T(512)}, u32[]{:S(2)}, u32[]{:S(2)}) collective-permute-start(s32[512]{0:T(512)} %concatenate.24), channel_id=1, source_target_pairs={{0,24},{4,28},{8,16},{12,20},{16,8},{20,12},{24,0},{28,4},{1,25},{... | collective-permute-start | bytes 6152 | tf_op jit(solution)/shard_map/ppermute | solution.py:27
  44.1 3.3 %collective-permute-start.5 = (s32[512]{0:T(512)}, s32[512]{0:T(512)}, u32[]{:S(2)}, u32[]{:S(2)}) collective-permute-start(s32[512]{0:T(512)} %concatenate.24), channel_id=1, source_target_pairs={{0,16},{4,20},{8,24},{12,28},{16,0},{20,4},{24,8},{28,12},{1,17},{... | collective-permute-start | bytes 6152 | tf_op jit(solution)/shard_map/ppermute | solution.py:27
  49.5 5.0 %collective-permute-done.6 = s32[512]{0:T(512)} collective-permute-done((s32[512]{0:T(512)}, s32[512]{0:T(512)}, u32[]{:S(2)}, u32[]{:S(2)}) %collective-permute-start.6) | collective-permute-done | bytes 2080 | tf_op jit(solution)/shard_map/ppermute | solution.py:27
  55.9 4.4 %assemble.1 = (bf16[1024,1024]{1,0:T(8,128)(2,1)}, bf16[1024,1024]{1,0:T(8,128)(2,1)}) custom-call(s32[2048]{0:T(1024)} %concatenate.25.code_ref, s32[3]{0:T(128)} %pad_add_fusion.1.place_ref, bf16[64,128,128]{2,1,0:T(8,128)(2,1)S(1)} %all-to-all-done.tile_ref), custom_call_target="tpu_custom_call" | custom-call | tf_op jit(solution)/shard_map/assemble/pallas_call | solution.py:93
  64.1 5.4 %collective-permute-done.13 = bf16[256,256]{1,0:T(8,128)(2,1)S(1)} collective-permute-done((bf16[256,256]{1,0:T(8,128)(2,1)S(1)}, bf16[256,256]{1,0:T(8,128)(2,1)S(1)}, u32[]{:S(2)}, u32[]{:S(2)}) %collective-permute-start.13) | collective-permute-done | bytes 131104 | tf_op jit(solution)/shard_map/ppermute | solution.py:27
  71.2 2.5 %collective-permute-done.11 = bf16[256,256]{1,0:T(8,128)(2,1)S(1)} collective-permute-done((bf16[256,256]{1,0:T(8,128)(2,1)S(1)}, bf16[256,256]{1,0:T(8,128)(2,1)S(1)}, u32[]{:S(2)}, u32[]{:S(2)}) %collective-permute-start.11) | collective-permute-done | bytes 131104 | tf_op jit(solution)/shard_map/ppermute | solution.py:27
  78.5 2.7 %project_part.2 = f32[256,256]{1,0:T(8,128)} custom-call(bf16[1024,256]{1,0:T(8,128)(2,1)S(1)} %copy-done.1, bf16[1024,256]{1,0:T(8,128)(2,1)S(1)} %copy-done.5, f32[1024,256]{1,0:T(8,128)S(1)} %fusion.70.refs_2_, f32[1024,256]{1,0:T(8,128)} %fusion.75.refs_3_, f32[256,256]{1,0:T(8,128)S(1)} %fusion.41.refs_4_), custom_call_target="tpu_custom_call" | custom-call | tf_op jit(solution)/shard_map/project_part/pallas_call | solution.py:121
  81.1 6.4 %all-to-all-start.1 = ((f32[32,8,256]{2,1,0:T(8,128)}), f32[32,8,256]{2,1,0:T(8,128)S(1)}, u32[]{:S(2)}, u32[]{:S(2)}) async-start(f32[32,8,256]{2,1,0:T(8,128)} %bitcast.55), calls=%async_computation.1 | async-start | bytes 524288 | tf_op jit(solution)/shard_map/all_to_all | solution.py:39
  89.9 6.1 %all-to-all-done.1 = f32[32,8,256]{2,1,0:T(8,128)S(1)} async-done(((f32[32,8,256]{2,1,0:T(8,128)}), f32[32,8,256]{2,1,0:T(8,128)S(1)}, u32[]{:S(2)}, u32[]{:S(2)}) %all-to-all-start.1) | async-done | bytes 262176 | tf_op jit(solution)/shard_map/all_to_all | solution.py:39
  96.7 4.9 %all-to-all-start.2 = ((f32[32,8,256]{2,1,0:T(8,128)}), f32[32,8,256]{2,1,0:T(8,128)S(1)}, u32[]{:S(2)}, u32[]{:S(2)}) async-start(f32[32,8,256]{2,1,0:T(8,128)} %broadcast_in_dim.8), calls=%async_computation.2 | async-start | bytes 524288 | tf_op jit(solution)/shard_map/all_to_all | solution.py:33
  105.3 3.7 %collective-permute-start.20 = (f32[256,256]{1,0:T(8,128)S(1)}, f32[256,256]{1,0:T(8,128)}, u32[]{:S(2)}, u32[]{:S(2)}) collective-permute-start(f32[256,256]{1,0:T(8,128)S(1)} %slice_add_fusion.3), channel_id=1, source_target_pairs={{0,16},{4,20},{8,24},{12,28},{16,0},{20,4},{24,8},{28,12},{1,17},{... | collective-permute-start | bytes 786440 | tf_op jit(solution)/shard_map/ppermute | solution.py:27
  111.2 2.3 %collective-permute-start.18 = (f32[256,256]{1,0:T(8,128)S(1)}, f32[256,256]{1,0:T(8,128)}, u32[]{:S(2)}, u32[]{:S(2)}) collective-permute-start(f32[256,256]{1,0:T(8,128)S(1)} %get-tuple-element.49), channel_id=1, source_target_pairs={{0,3},{1,2},{2,1},{3,0},{4,7},{5,6},{6,5},{7,4},{8,11},{9,10},{10,... | collective-permute-start | bytes 786440 | tf_op jit(solution)/shard_map/ppermute | solution.py:27
  114.9 4.2 %collective-permute-done.20 = f32[256,256]{1,0:T(8,128)} collective-permute-done((f32[256,256]{1,0:T(8,128)S(1)}, f32[256,256]{1,0:T(8,128)}, u32[]{:S(2)}, u32[]{:S(2)}) %collective-permute-start.20) | collective-permute-done | bytes 262176 | tf_op jit(solution)/shard_map/ppermute | solution.py:27
  119.8 4.5 %collective-permute-done.18 = f32[256,256]{1,0:T(8,128)} collective-permute-done((f32[256,256]{1,0:T(8,128)S(1)}, f32[256,256]{1,0:T(8,128)}, u32[]{:S(2)}, u32[]{:S(2)}) %collective-permute-start.18) | collective-permute-done | bytes 262176 | tf_op jit(solution)/shard_map/ppermute | solution.py:27
  127.3 8.7 %all_to_all.35 = f32[32,2,256]{2,1,0:T(2,128)S(1)} all-to-all(f32[32,2,256]{2,1,0:T(2,128)S(1)} %broadcast_in_dim.9), channel_id=1, replica_groups=mesh['row'=8,'col'=4] {'row','col'}, dimensions={0} | all-to-all | bytes 131072 | tf_op jit(solution)/shard_map/all_to_all | solution.py:33
  139.7 3.8 %collective-permute-done.26 = bf16[256,256]{1,0:T(8,128)(2,1)S(1)} collective-permute-done((bf16[256,256]{1,0:T(8,128)(2,1)S(1)}, bf16[256,256]{1,0:T(8,128)(2,1)S(1)}, u32[]{:S(2)}, u32[]{:S(2)}) %collective-permute-start.26) | collective-permute-done | bytes 131104 | tf_op jit(solution)/shard_map/ppermute | solution.py:27
  150.2 4.7 %collective-permute-done.23 = bf16[256,256]{1,0:T(8,128)(2,1)S(1)} collective-permute-done((bf16[256,256]{1,0:T(8,128)(2,1)S(1)}, bf16[256,256]{1,0:T(8,128)(2,1)S(1)}, u32[]{:S(2)}, u32[]{:S(2)}) %collective-permute-start.23) | collective-permute-done | bytes 131104 | tf_op jit(solution)/shard_map/ppermute | solution.py:27
  155.7 3.4 %collective-permute-done.21 = bf16[256,256]{1,0:T(8,128)(2,1)S(1)} collective-permute-done((bf16[256,256]{1,0:T(8,128)(2,1)S(1)}, bf16[256,256]{1,0:T(8,128)(2,1)S(1)}, u32[]{:S(2)}, u32[]{:S(2)}) %collective-permute-start.21) | collective-permute-done | bytes 131104 | tf_op jit(solution)/shard_map/ppermute | solution.py:27
  165.7 2.7 %project_part.3 = f32[256,256]{1,0:T(8,128)} custom-call(bf16[1024,256]{1,0:T(8,128)(2,1)S(1)} %copy-done.3, bf16[1024,256]{1,0:T(8,128)(2,1)S(1)} %copy-done.7, f32[1024,256]{1,0:T(8,128)S(1)} %fusion.76.refs_2_, f32[1024,256]{1,0:T(8,128)} %fusion.77.refs_3_, f32[256,256]{1,0:T(8,128)S(1)} %fusion.39.refs_4_), custom_call_target="tpu_custom_call" | custom-call | tf_op jit(solution)/shard_map/project_part/pallas_call | solution.py:121
  168.3 5.1 %all-to-all-start.4 = ((f32[32,8,256]{2,1,0:T(8,128)}), f32[32,8,256]{2,1,0:T(8,128)S(1)}, u32[]{:S(2)}, u32[]{:S(2)}) async-start(f32[32,8,256]{2,1,0:T(8,128)} %bitcast.54), calls=%async_computation.4 | async-start | bytes 524288 | tf_op jit(solution)/shard_map/all_to_all | solution.py:39
  176.2 5.6 %all-to-all-done.4 = f32[32,8,256]{2,1,0:T(8,128)S(1)} async-done(((f32[32,8,256]{2,1,0:T(8,128)}), f32[32,8,256]{2,1,0:T(8,128)S(1)}, u32[]{:S(2)}, u32[]{:S(2)}) %all-to-all-start.4) | async-done | bytes 262176 | tf_op jit(solution)/shard_map/all_to_all | solution.py:39
  182.6 4.9 %all-to-all-start.5 = ((f32[32,8,256]{2,1,0:T(8,128)}), f32[32,8,256]{2,1,0:T(8,128)S(1)}, u32[]{:S(2)}, u32[]{:S(2)}) async-start(f32[32,8,256]{2,1,0:T(8,128)} %broadcast_in_dim.10), calls=%async_computation.5 | async-start | bytes 524288 | tf_op jit(solution)/shard_map/all_to_all | solution.py:33
  187.4 3.6 %collective-permute-done.32 = f32[512,256]{1,0:T(8,128)S(1)} collective-permute-done((f32[512,256]{1,0:T(8,128)}, f32[512,256]{1,0:T(8,128)S(1)}, u32[]{:S(2)}, u32[]{:S(2)}) %collective-permute-start.32) | collective-permute-done | bytes 524320 | tf_op jit(solution)/shard_map/ppermute | solution.py:27
  191.8 3.6 %collective-permute-start.33 = (f32[256,256]{1,0:T(8,128)S(1)}, f32[256,256]{1,0:T(8,128)}, u32[]{:S(2)}, u32[]{:S(2)}) collective-permute-start(f32[256,256]{1,0:T(8,128)S(1)} %slice_add_fusion), channel_id=1, source_target_pairs={{0,16},{4,20},{8,24},{12,28},{16,0},{20,4},{24,8},{28,12},{1,17},{... | collective-permute-start | bytes 786440 | tf_op jit(solution)/shard_map/ppermute | solution.py:27
  200.6 4.9 %collective-permute-done.33 = f32[256,256]{1,0:T(8,128)} collective-permute-done((f32[256,256]{1,0:T(8,128)S(1)}, f32[256,256]{1,0:T(8,128)}, u32[]{:S(2)}, u32[]{:S(2)}) %collective-permute-start.33) | collective-permute-done | bytes 262176 | tf_op jit(solution)/shard_map/ppermute | solution.py:27
  207.1 3.8 %collective-permute-done.31 = f32[256,256]{1,0:T(8,128)} collective-permute-done((f32[256,256]{1,0:T(8,128)S(1)}, f32[256,256]{1,0:T(8,128)}, u32[]{:S(2)}, u32[]{:S(2)}) %collective-permute-start.31) | collective-permute-done | bytes 262176 | tf_op jit(solution)/shard_map/ppermute | solution.py:27
  214.3 3.3 %all-to-all-start.6 = ((f32[32,2,256]{2,1,0:T(2,128)}), f32[32,2,256]{2,1,0:T(2,128)S(1)}, u32[]{:S(2)}, u32[]{:S(2)}) async-start(f32[32,2,256]{2,1,0:T(2,128)} %broadcast_in_dim.11), calls=%async_computation.6 | async-start | bytes 131072 | tf_op jit(solution)/shard_map/all_to_all | solution.py:33
  218.4 4.4 %all-to-all-done.6 = f32[32,2,256]{2,1,0:T(2,128)S(1)} async-done(((f32[32,2,256]{2,1,0:T(2,128)}), f32[32,2,256]{2,1,0:T(2,128)S(1)}, u32[]{:S(2)}, u32[]{:S(2)}) %all-to-all-start.6) | async-done | bytes 65568 | tf_op jit(solution)/shard_map/all_to_all | solution.py:33
  (164 shorter events, 73.5 us)
Async XLA Ops:
  0.7 55.2 %all-to-all-start = ((bf16[64,128,128]{2,1,0:T(8,128)(2,1)}), bf16[64,128,128]{2,1,0:T(8,128)(2,1)S(1)}, u32[]{:S(2)}, u32[]{:S(2)}) async-start(bf16[64,128,128]{2,1,0:T(8,128)(2,1)} %param.6), calls=%async_computation | async-start | bytes 4194304 | tf_op jit(solution)/shard_map/all_to_all | solution.py:154
  7.5 18.7 %collective-permute-start.9 = (bf16[256,256]{1,0:T(8,128)(2,1)S(1)}, bf16[256,256]{1,0:T(8,128)(2,1)S(1)}, u32[]{:S(2)}, u32[]{:S(2)}) collective-permute-start(bf16[256,256]{1,0:T(8,128)(2,1)S(1)} %get-tuple-element.43), channel_id=1, source_target_pairs={{0,3},{1,2},{2,1},{3,0},{4,7},{5,6},{6,5},{7,4},{8,11},{9,10},{10,... | collective-permute-start | bytes 393224 | tf_op jit(solution)/shard_map/ppermute | solution.py:27
  8.9 20.9 %collective-permute-start.8 = (bf16[256,256]{1,0:T(8,128)(2,1)S(1)}, bf16[256,256]{1,0:T(8,128)(2,1)S(1)}, u32[]{:S(2)}, u32[]{:S(2)}) collective-permute-start(bf16[256,256]{1,0:T(8,128)(2,1)S(1)} %get-tuple-element.43), channel_id=1, source_target_pairs={{0,2},{1,3},{2,0},{3,1},{4,6},{5,7},{6,4},{7,5},{8,10},{9,11},{10,... | collective-permute-start | bytes 393224 | tf_op jit(solution)/shard_map/ppermute | solution.py:27
  9.5 20.3 %collective-permute-start.7 = (bf16[256,256]{1,0:T(8,128)(2,1)S(1)}, bf16[256,256]{1,0:T(8,128)(2,1)S(1)}, u32[]{:S(2)}, u32[]{:S(2)}) collective-permute-start(bf16[256,256]{1,0:T(8,128)(2,1)S(1)} %get-tuple-element.43), channel_id=1, source_target_pairs={{0,1},{1,0},{2,3},{3,2},{4,5},{5,4},{6,7},{7,6},{8,9},{9,8},{10,11... | collective-permute-start | bytes 393224 | tf_op jit(solution)/shard_map/ppermute | solution.py:27
  29.9 26.0 %collective-permute-start.10 = (bf16[1024,256]{1,0:T(8,128)(2,1)S(1)}, bf16[1024,256]{1,0:T(8,128)(2,1)S(1)}, u32[]{:S(2)}, u32[]{:S(2)}) collective-permute-start(bf16[1024,256]{1,0:T(8,128)(2,1)S(1)} %pad_maximum_fusion.refs_0_), channel_id=1, source_target_pairs={{0,4},{4,0},{8,12},{12,8},{16,20},{20,16},{24,28},{28,24},{1,5},{5... | collective-permute-start | bytes 1572872 | tf_op jit(solution)/shard_map/ppermute | solution.py:27
  40.1 14.4 %collective-permute-start.6 = (s32[512]{0:T(512)}, s32[512]{0:T(512)}, u32[]{:S(2)}, u32[]{:S(2)}) collective-permute-start(s32[512]{0:T(512)} %concatenate.24), channel_id=1, source_target_pairs={{0,24},{4,28},{8,16},{12,20},{16,8},{20,12},{24,0},{28,4},{1,25},{... | collective-permute-start | bytes 6152 | tf_op jit(solution)/shard_map/ppermute | solution.py:27
  44.1 10.4 %collective-permute-start.5 = (s32[512]{0:T(512)}, s32[512]{0:T(512)}, u32[]{:S(2)}, u32[]{:S(2)}) collective-permute-start(s32[512]{0:T(512)} %concatenate.24), channel_id=1, source_target_pairs={{0,16},{4,20},{8,24},{12,28},{16,0},{20,4},{24,8},{28,12},{1,17},{... | collective-permute-start | bytes 6152 | tf_op jit(solution)/shard_map/ppermute | solution.py:27
  60.3 13.5 %collective-permute-start.14 = (bf16[1024,1024]{1,0:T(8,128)(2,1)}, bf16[1024,1024]{1,0:T(8,128)(2,1)S(1)}, u32[]{:S(2)}, u32[]{:S(2)}) collective-permute-start(bf16[1024,1024]{1,0:T(8,128)(2,1)} %get-tuple-element.24), channel_id=1, source_target_pairs={{0,4},{4,0},{8,12},{12,8},{16,20},{20,16},{24,28},{28,24},{1,5},{5... | collective-permute-start | bytes 6291464 | tf_op jit(solution)/shard_map/ppermute | solution.py:27
  60.3 9.2 %collective-permute-start.13 = (bf16[256,256]{1,0:T(8,128)(2,1)S(1)}, bf16[256,256]{1,0:T(8,128)(2,1)S(1)}, u32[]{:S(2)}, u32[]{:S(2)}) collective-permute-start(bf16[256,256]{1,0:T(8,128)(2,1)S(1)} %get-tuple-element.51), channel_id=1, source_target_pairs={{0,24},{4,28},{8,16},{12,20},{16,8},{20,12},{24,0},{28,4},{1,25},{... | collective-permute-start | bytes 393224 | tf_op jit(solution)/shard_map/ppermute | solution.py:27
  61.2 10.1 %collective-permute-start.12 = (bf16[256,256]{1,0:T(8,128)(2,1)S(1)}, bf16[256,256]{1,0:T(8,128)(2,1)S(1)}, u32[]{:S(2)}, u32[]{:S(2)}) collective-permute-start(bf16[256,256]{1,0:T(8,128)(2,1)S(1)} %get-tuple-element.51), channel_id=1, source_target_pairs={{0,8},{4,12},{8,0},{12,4},{16,24},{20,28},{24,16},{28,20},{1,9},{5... | collective-permute-start | bytes 393224 | tf_op jit(solution)/shard_map/ppermute | solution.py:27
  63.4 10.4 %collective-permute-start.11 = (bf16[256,256]{1,0:T(8,128)(2,1)S(1)}, bf16[256,256]{1,0:T(8,128)(2,1)S(1)}, u32[]{:S(2)}, u32[]{:S(2)}) collective-permute-start(bf16[256,256]{1,0:T(8,128)(2,1)S(1)} %get-tuple-element.51), channel_id=1, source_target_pairs={{0,16},{4,20},{8,24},{12,28},{16,0},{20,4},{24,8},{28,12},{1,17},{... | collective-permute-start | bytes 393224 | tf_op jit(solution)/shard_map/ppermute | solution.py:27
  77.3 31.7 %collective-permute-start.15 = (f32[1024,256]{1,0:T(8,128)}, f32[1024,256]{1,0:T(8,128)}, u32[]{:S(2)}, u32[]{:S(2)}) collective-permute-start(f32[1024,256]{1,0:T(8,128)} %fusion.75.refs_3_), channel_id=1, source_target_pairs={{0,4},{4,0},{8,12},{12,8},{16,20},{20,16},{24,28},{28,24},{1,5},{5... | collective-permute-start | bytes 3145736 | tf_op jit(solution)/shard_map/ppermute | solution.py:27
  81.1 14.8 %all-to-all-start.1 = ((f32[32,8,256]{2,1,0:T(8,128)}), f32[32,8,256]{2,1,0:T(8,128)S(1)}, u32[]{:S(2)}, u32[]{:S(2)}) async-start(f32[32,8,256]{2,1,0:T(8,128)} %bitcast.55), calls=%async_computation.1 | async-start | bytes 524288 | tf_op jit(solution)/shard_map/all_to_all | solution.py:39
  87.6 17.6 %collective-permute-start.19 = (f32[512,256]{1,0:T(8,128)}, f32[512,256]{1,0:T(8,128)S(1)}, u32[]{:S(2)}, u32[]{:S(2)}) collective-permute-start(f32[512,256]{1,0:T(8,128)} %convolution_add_fusion.3), channel_id=1, source_target_pairs={{0,8},{4,12},{8,0},{12,4},{16,24},{20,28},{24,16},{28,20},{1,9},{5... | collective-permute-start | bytes 1572872 | tf_op jit(solution)/shard_map/ppermute | solution.py:27
  96.7 17.3 %all-to-all-start.2 = ((f32[32,8,256]{2,1,0:T(8,128)}), f32[32,8,256]{2,1,0:T(8,128)S(1)}, u32[]{:S(2)}, u32[]{:S(2)}) async-start(f32[32,8,256]{2,1,0:T(8,128)} %broadcast_in_dim.8), calls=%async_computation.2 | async-start | bytes 524288 | tf_op jit(solution)/shard_map/all_to_all | solution.py:33
  105.3 13.8 %collective-permute-start.20 = (f32[256,256]{1,0:T(8,128)S(1)}, f32[256,256]{1,0:T(8,128)}, u32[]{:S(2)}, u32[]{:S(2)}) collective-permute-start(f32[256,256]{1,0:T(8,128)S(1)} %slice_add_fusion.3), channel_id=1, source_target_pairs={{0,16},{4,20},{8,24},{12,28},{16,0},{20,4},{24,8},{28,12},{1,17},{... | collective-permute-start | bytes 786440 | tf_op jit(solution)/shard_map/ppermute | solution.py:27
  110.5 9.4 %collective-permute-start.16 = (f32[256,256]{1,0:T(8,128)S(1)}, f32[256,256]{1,0:T(8,128)}, u32[]{:S(2)}, u32[]{:S(2)}) collective-permute-start(f32[256,256]{1,0:T(8,128)S(1)} %get-tuple-element.48), channel_id=1, source_target_pairs={{0,1},{1,0},{2,3},{3,2},{4,5},{5,4},{6,7},{7,6},{8,9},{9,8},{10,11... | collective-permute-start | bytes 786440 | tf_op jit(solution)/shard_map/ppermute | solution.py:27
  111.2 13.0 %collective-permute-start.18 = (f32[256,256]{1,0:T(8,128)S(1)}, f32[256,256]{1,0:T(8,128)}, u32[]{:S(2)}, u32[]{:S(2)}) collective-permute-start(f32[256,256]{1,0:T(8,128)S(1)} %get-tuple-element.49), channel_id=1, source_target_pairs={{0,3},{1,2},{2,1},{3,0},{4,7},{5,6},{6,5},{7,4},{8,11},{9,10},{10,... | collective-permute-start | bytes 786440 | tf_op jit(solution)/shard_map/ppermute | solution.py:27
  113.6 12.1 %collective-permute-start.17 = (f32[256,256]{1,0:T(8,128)S(1)}, f32[256,256]{1,0:T(8,128)}, u32[]{:S(2)}, u32[]{:S(2)}) collective-permute-start(f32[256,256]{1,0:T(8,128)S(1)} %get-tuple-element.50), channel_id=1, source_target_pairs={{0,2},{1,3},{2,0},{3,1},{4,6},{5,7},{6,4},{7,5},{8,10},{9,11},{10,... | collective-permute-start | bytes 786440 | tf_op jit(solution)/shard_map/ppermute | solution.py:27
  145.5 13.6 %collective-permute-start.27 = (bf16[1024,256]{1,0:T(8,128)(2,1)S(1)}, bf16[1024,256]{1,0:T(8,128)(2,1)S(1)}, u32[]{:S(2)}, u32[]{:S(2)}) collective-permute-start(bf16[1024,256]{1,0:T(8,128)(2,1)S(1)} %pad_maximum_fusion.2.refs_0_), channel_id=1, source_target_pairs={{0,4},{4,0},{8,12},{12,8},{16,20},{20,16},{24,28},{28,24},{1,5},{5... | collective-permute-start | bytes 1572872 | tf_op jit(solution)/shard_map/ppermute | solution.py:27
  145.6 9.2 %collective-permute-start.23 = (bf16[256,256]{1,0:T(8,128)(2,1)S(1)}, bf16[256,256]{1,0:T(8,128)(2,1)S(1)}, u32[]{:S(2)}, u32[]{:S(2)}) collective-permute-start(bf16[256,256]{1,0:T(8,128)(2,1)S(1)} %fusion.69), channel_id=1, source_target_pairs={{0,24},{4,28},{8,16},{12,20},{16,8},{20,12},{24,0},{28,4},{1,25},{... | collective-permute-start | bytes 393224 | tf_op jit(solution)/shard_map/ppermute | solution.py:27
  146.3 9.4 %collective-permute-start.22 = (bf16[256,256]{1,0:T(8,128)(2,1)S(1)}, bf16[256,256]{1,0:T(8,128)(2,1)S(1)}, u32[]{:S(2)}, u32[]{:S(2)}) collective-permute-start(bf16[256,256]{1,0:T(8,128)(2,1)S(1)} %fusion.69), channel_id=1, source_target_pairs={{0,8},{4,12},{8,0},{12,4},{16,24},{20,28},{24,16},{28,20},{1,9},{5... | collective-permute-start | bytes 393224 | tf_op jit(solution)/shard_map/ppermute | solution.py:27
  148.0 11.1 %collective-permute-start.21 = (bf16[256,256]{1,0:T(8,128)(2,1)S(1)}, bf16[256,256]{1,0:T(8,128)(2,1)S(1)}, u32[]{:S(2)}, u32[]{:S(2)}) collective-permute-start(bf16[256,256]{1,0:T(8,128)(2,1)S(1)} %fusion.69), channel_id=1, source_target_pairs={{0,16},{4,20},{8,24},{12,28},{16,0},{20,4},{24,8},{28,12},{1,17},{... | collective-permute-start | bytes 393224 | tf_op jit(solution)/shard_map/ppermute | solution.py:27
  165.7 29.9 %collective-permute-start.28 = (f32[1024,256]{1,0:T(8,128)}, f32[1024,256]{1,0:T(8,128)}, u32[]{:S(2)}, u32[]{:S(2)}) collective-permute-start(f32[1024,256]{1,0:T(8,128)} %fusion.77.refs_3_), channel_id=1, source_target_pairs={{0,4},{4,0},{8,12},{12,8},{16,20},{20,16},{24,28},{28,24},{1,5},{5... | collective-permute-start | bytes 3145736 | tf_op jit(solution)/shard_map/ppermute | solution.py:27
  168.3 13.5 %all-to-all-start.4 = ((f32[32,8,256]{2,1,0:T(8,128)}), f32[32,8,256]{2,1,0:T(8,128)S(1)}, u32[]{:S(2)}, u32[]{:S(2)}) async-start(f32[32,8,256]{2,1,0:T(8,128)} %bitcast.54), calls=%async_computation.4 | async-start | bytes 524288 | tf_op jit(solution)/shard_map/all_to_all | solution.py:39
  173.4 17.6 %collective-permute-start.32 = (f32[512,256]{1,0:T(8,128)}, f32[512,256]{1,0:T(8,128)S(1)}, u32[]{:S(2)}, u32[]{:S(2)}) collective-permute-start(f32[512,256]{1,0:T(8,128)} %convolution_add_fusion.1), channel_id=1, source_target_pairs={{0,8},{4,12},{8,0},{12,4},{16,24},{20,28},{24,16},{28,20},{1,9},{5... | collective-permute-start | bytes 1572872 | tf_op jit(solution)/shard_map/ppermute | solution.py:27
  182.6 22.9 %all-to-all-start.5 = ((f32[32,8,256]{2,1,0:T(8,128)}), f32[32,8,256]{2,1,0:T(8,128)S(1)}, u32[]{:S(2)}, u32[]{:S(2)}) async-start(f32[32,8,256]{2,1,0:T(8,128)} %broadcast_in_dim.10), calls=%async_computation.5 | async-start | bytes 524288 | tf_op jit(solution)/shard_map/all_to_all | solution.py:33
  191.8 13.7 %collective-permute-start.33 = (f32[256,256]{1,0:T(8,128)S(1)}, f32[256,256]{1,0:T(8,128)}, u32[]{:S(2)}, u32[]{:S(2)}) collective-permute-start(f32[256,256]{1,0:T(8,128)S(1)} %slice_add_fusion), channel_id=1, source_target_pairs={{0,16},{4,20},{8,24},{12,28},{16,0},{20,4},{24,8},{28,12},{1,17},{... | collective-permute-start | bytes 786440 | tf_op jit(solution)/shard_map/ppermute | solution.py:27
  197.0 10.0 %collective-permute-start.29 = (f32[256,256]{1,0:T(8,128)S(1)}, f32[256,256]{1,0:T(8,128)S(1)}, u32[]{:S(2)}, u32[]{:S(2)}) collective-permute-start(f32[256,256]{1,0:T(8,128)S(1)} %get-tuple-element.45), channel_id=1, source_target_pairs={{0,1},{1,0},{2,3},{3,2},{4,5},{5,4},{6,7},{7,6},{8,9},{9,8},{10,11... | collective-permute-start | bytes 786440 | tf_op jit(solution)/shard_map/ppermute | solution.py:27
  197.8 13.0 %collective-permute-start.31 = (f32[256,256]{1,0:T(8,128)S(1)}, f32[256,256]{1,0:T(8,128)}, u32[]{:S(2)}, u32[]{:S(2)}) collective-permute-start(f32[256,256]{1,0:T(8,128)S(1)} %get-tuple-element.46), channel_id=1, source_target_pairs={{0,3},{1,2},{2,1},{3,0},{4,7},{5,6},{6,5},{7,4},{8,11},{9,10},{10,... | collective-permute-start | bytes 786440 | tf_op jit(solution)/shard_map/ppermute | solution.py:27
  200.1 12.1 %collective-permute-start.30 = (f32[256,256]{1,0:T(8,128)S(1)}, f32[256,256]{1,0:T(8,128)}, u32[]{:S(2)}, u32[]{:S(2)}) collective-permute-start(f32[256,256]{1,0:T(8,128)S(1)} %get-tuple-element.47), channel_id=1, source_target_pairs={{0,2},{1,3},{2,0},{3,1},{4,6},{5,7},{6,4},{7,5},{8,10},{9,11},{10,... | collective-permute-start | bytes 786440 | tf_op jit(solution)/shard_map/ppermute | solution.py:27
  214.3 8.6 %all-to-all-start.6 = ((f32[32,2,256]{2,1,0:T(2,128)}), f32[32,2,256]{2,1,0:T(2,128)S(1)}, u32[]{:S(2)}, u32[]{:S(2)}) async-start(f32[32,2,256]{2,1,0:T(2,128)} %broadcast_in_dim.11), calls=%async_computation.6 | async-start | bytes 131072 | tf_op jit(solution)/shard_map/all_to_all | solution.py:33
  (38 other events, 396.1 us)

commit v4 on v3

--- a/solution.py
+++ b/solution.py
@@ -149,7 +149,7 @@
         left_bf = scaled_left.astype(bf16)
         diag_right = diag_col * right_vec
         right_all, left_own, left_sib = gather(right_bf, left_bf)
-        local_proj = lax.dot_general(scaled_left, diag_right, FIRST, precision=lax.Precision.HIGHEST)
+        local_proj = lax.dot_general(scaled_left, diag_right, FIRST, precision=lax.Precision.HIGH)
         if turn == 0:
             got_tiles = lax.all_to_all(tile_values, AXES, split_axis=0, concat_axis=0, tiled=True)
             codes = slot_codes
@@ -161,10 +161,6 @@
             (got_tiles,) = in_vmem(got_tiles)
             own_half, sib_half = assemble(got_tiles, codes, place, levels, col_size)
             other_half = partner(sib_half, "row", 1)
-        else:
-            right_all, left_own, left_sib, local_proj = lax.optimization_barrier(
-                (right_all, left_own, left_sib, local_proj)
-            )
         right_all = jnp.concatenate(right_all, axis=0)
         half = levels * rows // 2
 
@@ -199,8 +195,8 @@
             right_prod += partner(right_pair[k * rows : (k + 1) * rows], "col", k)
         right_new = scale_col * (right_prod + diag_right)
         left_new = left_prod + diag_col * scaled_left
-        right_rest = right_new - jnp.dot(right_vec, project, precision=lax.Precision.HIGHEST)
-        left_rest = left_new - jnp.dot(left_vec, project.T, precision=lax.Precision.HIGHEST)
+        right_rest = right_new - jnp.dot(right_vec, project, precision=lax.Precision.HIGH)
+        left_rest = left_new - jnp.dot(left_vec, project.T, precision=lax.Precision.HIGH)
         squares = jnp.stack(
             [jnp.sum(right_rest * right_rest, axis=0), jnp.sum(left_rest * left_rest, axis=0)]
         )

time: 228 us -> 228 us (level)
  no operation moved by 1% of the time
where the time goes in v4:
time: 228 us; the launch traced here: 224 us
  waiting for transfers between devices  93.2 us (41%)
  starting transfers between devices  73.7 us (32%)
  matrix products  19.4 us (9%)
  Pallas kernels  9.66 us (4%)
  other arithmetic  9.15 us (4%)
  blocking collectives  8.72 us (4%)
  local copies, waits for them, and re-layouts  8.35 us (4%)
    ppermute x34, waiting for transfers between devices, partner(): lax.ppermute(value, axis, [(index, index ^ offset) for index in range(siz...  77.1 us
    ppermute x34, starting transfers between devices, partner(): lax.ppermute(value, axis, [(index, index ^ offset) for index in range(siz...  42.9 us
    all_to_all x3, starting transfers between devices, copies_of_all(): return lax.all_to_all(copies, AXES, split_axis=0, concat_axis=0, tiled=True)  13.2 us
    all_to_all x2, waiting for transfers between devices, sum_over_all(): lax.all_to_all(pieces, AXES, split_axis=0, concat_axis=0, tiled=True)  11.7 us
    all_to_all x2, starting transfers between devices, sum_over_all(): lax.all_to_all(pieces, AXES, split_axis=0, concat_axis=0, tiled=True)  11.5 us
    all_to_all x1, blocking collectives, copies_of_all(): return lax.all_to_all(copies, AXES, split_axis=0, concat_axis=0, tiled=True)  8.72 us
    all_to_all x1, starting transfers between devices, local(): lax.all_to_all(tile_values, AXES, split_axis=0, concat_axis=0, tiled=True)  6.02 us
    pallas_call x2, Pallas kernels, project_part(): pl.pallas_call(kernel, out_shape=jax.ShapeDtypeStruct((ports, ports), f32...  5.32 us
  transfers between devices with their start and end apart: 40, of which 25 were waited for; matrix products, arithmetic and copies ran while one was open for 10% of the time, Pallas kernels for 2%

profile of v4, /device:TPU:10, one launch (start us, length us, event | category | flops | bytes accessed | tf_op | source)
XLA Modules:
  0.0 223.6 jit_solution(4753277087383439134)
XLA Ops:
  0.7 6.0 %all-to-all-start = ((bf16[64,128,128]{2,1,0:T(8,128)(2,1)}), bf16[64,128,128]{2,1,0:T(8,128)(2,1)S(1)}, u32[]{:S(2)}, u32[]{:S(2)}) async-start(bf16[64,128,128]{2,1,0:T(8,128)(2,1)} %param.6), calls=%async_computation | async-start | bytes 4194304 | tf_op jit(solution)/shard_map/all_to_all | solution.py:154
  11.0 15.2 %collective-permute-done.9 = bf16[256,256]{1,0:T(8,128)(2,1)S(1)} collective-permute-done((bf16[256,256]{1,0:T(8,128)(2,1)S(1)}, bf16[256,256]{1,0:T(8,128)(2,1)S(1)}, u32[]{:S(2)}, u32[]{:S(2)}) %collective-permute-start.9) | collective-permute-done | bytes 131104 | tf_op jit(solution)/shard_map/ppermute | solution.py:27
  26.1 3.7 %collective-permute-done.8 = bf16[256,256]{1,0:T(8,128)(2,1)S(1)} collective-permute-done((bf16[256,256]{1,0:T(8,128)(2,1)S(1)}, bf16[256,256]{1,0:T(8,128)(2,1)S(1)}, u32[]{:S(2)}, u32[]{:S(2)}) %collective-permute-start.8) | collective-permute-done | bytes 131104 | tf_op jit(solution)/shard_map/ppermute | solution.py:27
  30.1 2.3 %collective-permute-start.1 = (s32[64]{0:T(128)S(1)}, s32[64]{0:T(128)S(1)}, u32[]{:S(2)}, u32[]{:S(2)}) collective-permute-start(s32[64]{0:T(128)S(1)} %copy-done.29), channel_id=1, source_target_pairs={{0,2},{1,3},{2,0},{3,1},{4,6},{5,7},{6,4},{7,5},{8,10},{9,11},{10,... | collective-permute-start | bytes 776 | tf_op jit(solution)/shard_map/ppermute | solution.py:27
  40.2 4.1 %collective-permute-start.6 = (s32[512]{0:T(512)}, s32[512]{0:T(512)}, u32[]{:S(2)}, u32[]{:S(2)}) collective-permute-start(s32[512]{0:T(512)} %concatenate.24), channel_id=1, source_target_pairs={{0,24},{4,28},{8,16},{12,20},{16,8},{20,12},{24,0},{28,4},{1,25},{... | collective-permute-start | bytes 6152 | tf_op jit(solution)/shard_map/ppermute | solution.py:27
  44.2 3.3 %collective-permute-start.5 = (s32[512]{0:T(512)}, s32[512]{0:T(512)}, u32[]{:S(2)}, u32[]{:S(2)}) collective-permute-start(s32[512]{0:T(512)} %concatenate.24), channel_id=1, source_target_pairs={{0,16},{4,20},{8,24},{12,28},{16,0},{20,4},{24,8},{28,12},{1,17},{... | collective-permute-start | bytes 6152 | tf_op jit(solution)/shard_map/ppermute | solution.py:27
  49.6 4.9 %collective-permute-done.6 = s32[512]{0:T(512)} collective-permute-done((s32[512]{0:T(512)}, s32[512]{0:T(512)}, u32[]{:S(2)}, u32[]{:S(2)}) %collective-permute-start.6) | collective-permute-done | bytes 2080 | tf_op jit(solution)/shard_map/ppermute | solution.py:27
  55.9 4.3 %assemble.1 = (bf16[1024,1024]{1,0:T(8,128)(2,1)}, bf16[1024,1024]{1,0:T(8,128)(2,1)}) custom-call(s32[2048]{0:T(1024)} %concatenate.25.code_ref, s32[3]{0:T(128)} %pad_add_fusion.1.place_ref, bf16[64,128,128]{2,1,0:T(8,128)(2,1)S(1)} %all-to-all-done.tile_ref), custom_call_target="tpu_custom_call" | custom-call | tf_op jit(solution)/shard_map/assemble/pallas_call | solution.py:93
  64.0 5.4 %collective-permute-done.14 = bf16[256,256]{1,0:T(8,128)(2,1)S(1)} collective-permute-done((bf16[256,256]{1,0:T(8,128)(2,1)S(1)}, bf16[256,256]{1,0:T(8,128)(2,1)S(1)}, u32[]{:S(2)}, u32[]{:S(2)}) %collective-permute-start.14) | collective-permute-done | bytes 131104 | tf_op jit(solution)/shard_map/ppermute | solution.py:27
  71.2 2.5 %collective-permute-done.12 = bf16[256,256]{1,0:T(8,128)(2,1)S(1)} collective-permute-done((bf16[256,256]{1,0:T(8,128)(2,1)S(1)}, bf16[256,256]{1,0:T(8,128)(2,1)S(1)}, u32[]{:S(2)}, u32[]{:S(2)}) %collective-permute-start.12) | collective-permute-done | bytes 131104 | tf_op jit(solution)/shard_map/ppermute | solution.py:27
  78.5 2.7 %project_part.2 = f32[256,256]{1,0:T(8,128)} custom-call(bf16[1024,256]{1,0:T(8,128)(2,1)S(1)} %copy-done.1, bf16[1024,256]{1,0:T(8,128)(2,1)S(1)} %copy-done.5, f32[1024,256]{1,0:T(8,128)S(1)} %fusion.70.refs_2_, f32[1024,256]{1,0:T(8,128)} %fusion.75.refs_3_, f32[256,256]{1,0:T(8,128)S(1)} %fusion.41.refs_4_), custom_call_target="tpu_custom_call" | custom-call | tf_op jit(solution)/shard_map/project_part/pallas_call | solution.py:121
  81.2 6.4 %all-to-all-start.1 = ((f32[32,8,256]{2,1,0:T(8,128)}), f32[32,8,256]{2,1,0:T(8,128)S(1)}, u32[]{:S(2)}, u32[]{:S(2)}) async-start(f32[32,8,256]{2,1,0:T(8,128)} %bitcast.53), calls=%async_computation.1 | async-start | bytes 524288 | tf_op jit(solution)/shard_map/all_to_all | solution.py:39
  89.9 6.1 %all-to-all-done.1 = f32[32,8,256]{2,1,0:T(8,128)S(1)} async-done(((f32[32,8,256]{2,1,0:T(8,128)}), f32[32,8,256]{2,1,0:T(8,128)S(1)}, u32[]{:S(2)}, u32[]{:S(2)}) %all-to-all-start.1) | async-done | bytes 262176 | tf_op jit(solution)/shard_map/all_to_all | solution.py:39
  96.7 4.9 %all-to-all-start.2 = ((f32[32,8,256]{2,1,0:T(8,128)}), f32[32,8,256]{2,1,0:T(8,128)S(1)}, u32[]{:S(2)}, u32[]{:S(2)}) async-start(f32[32,8,256]{2,1,0:T(8,128)} %broadcast_in_dim.8), calls=%async_computation.2 | async-start | bytes 524288 | tf_op jit(solution)/shard_map/all_to_all | solution.py:33
  105.3 3.7 %collective-permute-start.16 = (f32[256,256]{1,0:T(8,128)S(1)}, f32[256,256]{1,0:T(8,128)}, u32[]{:S(2)}, u32[]{:S(2)}) collective-permute-start(f32[256,256]{1,0:T(8,128)S(1)} %slice_add_fusion.4), channel_id=1, source_target_pairs={{0,16},{4,20},{8,24},{12,28},{16,0},{20,4},{24,8},{28,12},{1,17},{... | collective-permute-start | bytes 786440 | tf_op jit(solution)/shard_map/ppermute | solution.py:27
  114.7 4.4 %collective-permute-done.16 = f32[256,256]{1,0:T(8,128)} collective-permute-done((f32[256,256]{1,0:T(8,128)S(1)}, f32[256,256]{1,0:T(8,128)}, u32[]{:S(2)}, u32[]{:S(2)}) %collective-permute-start.16) | collective-permute-done | bytes 262176 | tf_op jit(solution)/shard_map/ppermute | solution.py:27
  119.8 4.5 %collective-permute-done.20 = f32[256,256]{1,0:T(8,128)} collective-permute-done((f32[256,256]{1,0:T(8,128)S(1)}, f32[256,256]{1,0:T(8,128)}, u32[]{:S(2)}, u32[]{:S(2)}) %collective-permute-start.20) | collective-permute-done | bytes 262176 | tf_op jit(solution)/shard_map/ppermute | solution.py:27
  127.3 8.7 %all_to_all.35 = f32[32,2,256]{2,1,0:T(2,128)S(1)} all-to-all(f32[32,2,256]{2,1,0:T(2,128)S(1)} %broadcast_in_dim.9), channel_id=1, replica_groups=mesh['row'=8,'col'=4] {'row','col'}, dimensions={0} | all-to-all | bytes 131072 | tf_op jit(solution)/shard_map/all_to_all | solution.py:33
  139.7 3.8 %collective-permute-done.23 = bf16[256,256]{1,0:T(8,128)(2,1)S(1)} collective-permute-done((bf16[256,256]{1,0:T(8,128)(2,1)S(1)}, bf16[256,256]{1,0:T(8,128)(2,1)S(1)}, u32[]{:S(2)}, u32[]{:S(2)}) %collective-permute-start.23) | collective-permute-done | bytes 131104 | tf_op jit(solution)/shard_map/ppermute | solution.py:27
  150.8 4.9 %collective-permute-done.27 = bf16[256,256]{1,0:T(8,128)(2,1)S(1)} collective-permute-done((bf16[256,256]{1,0:T(8,128)(2,1)S(1)}, bf16[256,256]{1,0:T(8,128)(2,1)S(1)}, u32[]{:S(2)}, u32[]{:S(2)}) %collective-permute-start.27) | collective-permute-done | bytes 131104 | tf_op jit(solution)/shard_map/ppermute | solution.py:27
  156.5 3.4 %collective-permute-done.25 = bf16[256,256]{1,0:T(8,128)(2,1)S(1)} collective-permute-done((bf16[256,256]{1,0:T(8,128)(2,1)S(1)}, bf16[256,256]{1,0:T(8,128)(2,1)S(1)}, u32[]{:S(2)}, u32[]{:S(2)}) %collective-permute-start.25) | collective-permute-done | bytes 131104 | tf_op jit(solution)/shard_map/ppermute | solution.py:27
  165.5 2.7 %project_part.3 = f32[256,256]{1,0:T(8,128)} custom-call(bf16[1024,256]{1,0:T(8,128)(2,1)S(1)} %copy-done.3, bf16[1024,256]{1,0:T(8,128)(2,1)S(1)} %copy-done.7, f32[1024,256]{1,0:T(8,128)S(1)} %fusion.76.refs_2_, f32[1024,256]{1,0:T(8,128)} %fusion.77.refs_3_, f32[256,256]{1,0:T(8,128)S(1)} %fusion.39.refs_4_), custom_call_target="tpu_custom_call" | custom-call | tf_op jit(solution)/shard_map/project_part/pallas_call | solution.py:121
  168.1 5.1 %all-to-all-start.4 = ((f32[32,8,256]{2,1,0:T(8,128)}), f32[32,8,256]{2,1,0:T(8,128)S(1)}, u32[]{:S(2)}, u32[]{:S(2)}) async-start(f32[32,8,256]{2,1,0:T(8,128)} %bitcast.52), calls=%async_computation.4 | async-start | bytes 524288 | tf_op jit(solution)/shard_map/all_to_all | solution.py:39
  176.1 5.6 %all-to-all-done.4 = f32[32,8,256]{2,1,0:T(8,128)S(1)} async-done(((f32[32,8,256]{2,1,0:T(8,128)}), f32[32,8,256]{2,1,0:T(8,128)S(1)}, u32[]{:S(2)}, u32[]{:S(2)}) %all-to-all-start.4) | async-done | bytes 262176 | tf_op jit(solution)/shard_map/all_to_all | solution.py:39
  182.5 4.9 %all-to-all-start.5 = ((f32[32,8,256]{2,1,0:T(8,128)}), f32[32,8,256]{2,1,0:T(8,128)S(1)}, u32[]{:S(2)}, u32[]{:S(2)}) async-start(f32[32,8,256]{2,1,0:T(8,128)} %broadcast_in_dim.10), calls=%async_computation.5 | async-start | bytes 524288 | tf_op jit(solution)/shard_map/all_to_all | solution.py:33
  187.4 3.5 %collective-permute-done.32 = f32[512,256]{1,0:T(8,128)S(1)} collective-permute-done((f32[512,256]{1,0:T(8,128)}, f32[512,256]{1,0:T(8,128)S(1)}, u32[]{:S(2)}, u32[]{:S(2)}) %collective-permute-start.32) | collective-permute-done | bytes 524320 | tf_op jit(solution)/shard_map/ppermute | solution.py:27
  191.6 3.6 %collective-permute-start.33 = (f32[256,256]{1,0:T(8,128)S(1)}, f32[256,256]{1,0:T(8,128)}, u32[]{:S(2)}, u32[]{:S(2)}) collective-permute-start(f32[256,256]{1,0:T(8,128)S(1)} %slice_add_fusion), channel_id=1, source_target_pairs={{0,16},{4,20},{8,24},{12,28},{16,0},{20,4},{24,8},{28,12},{1,17},{... | collective-permute-start | bytes 786440 | tf_op jit(solution)/shard_map/ppermute | solution.py:27
  197.6 2.4 %collective-permute-start.31 = (f32[256,256]{1,0:T(8,128)S(1)}, f32[256,256]{1,0:T(8,128)}, u32[]{:S(2)}, u32[]{:S(2)}) collective-permute-start(f32[256,256]{1,0:T(8,128)S(1)} %get-tuple-element.32), channel_id=1, source_target_pairs={{0,3},{1,2},{2,1},{3,0},{4,7},{5,6},{6,5},{7,4},{8,11},{9,10},{10,... | collective-permute-start | bytes 786440 | tf_op jit(solution)/shard_map/ppermute | solution.py:27
  200.4 5.1 %collective-permute-done.33 = f32[256,256]{1,0:T(8,128)} collective-permute-done((f32[256,256]{1,0:T(8,128)S(1)}, f32[256,256]{1,0:T(8,128)}, u32[]{:S(2)}, u32[]{:S(2)}) %collective-permute-start.33) | collective-permute-done | bytes 262176 | tf_op jit(solution)/shard_map/ppermute | solution.py:27
  206.9 3.6 %collective-permute-done.31 = f32[256,256]{1,0:T(8,128)} collective-permute-done((f32[256,256]{1,0:T(8,128)S(1)}, f32[256,256]{1,0:T(8,128)}, u32[]{:S(2)}, u32[]{:S(2)}) %collective-permute-start.31) | collective-permute-done | bytes 262176 | tf_op jit(solution)/shard_map/ppermute | solution.py:27
  213.9 3.5 %all-to-all-start.6 = ((f32[32,2,256]{2,1,0:T(2,128)}), f32[32,2,256]{2,1,0:T(2,128)S(1)}, u32[]{:S(2)}, u32[]{:S(2)}) async-start(f32[32,2,256]{2,1,0:T(2,128)} %broadcast_in_dim.11), calls=%async_computation.6 | async-start | bytes 131072 | tf_op jit(solution)/shard_map/all_to_all | solution.py:33
  218.3 4.4 %all-to-all-done.6 = f32[32,2,256]{2,1,0:T(2,128)S(1)} async-done(((f32[32,2,256]{2,1,0:T(2,128)}), f32[32,2,256]{2,1,0:T(2,128)S(1)}, u32[]{:S(2)}, u32[]{:S(2)}) %all-to-all-start.6) | async-done | bytes 65568 | tf_op jit(solution)/shard_map/all_to_all | solution.py:33
  (176 shorter events, 72.8 us)
Async XLA Ops:
  0.7 55.2 %all-to-all-start = ((bf16[64,128,128]{2,1,0:T(8,128)(2,1)}), bf16[64,128,128]{2,1,0:T(8,128)(2,1)S(1)}, u32[]{:S(2)}, u32[]{:S(2)}) async-start(bf16[64,128,128]{2,1,0:T(8,128)(2,1)} %param.6), calls=%async_computation | async-start | bytes 4194304 | tf_op jit(solution)/shard_map/all_to_all | solution.py:154
  7.5 18.7 %collective-permute-start.9 = (bf16[256,256]{1,0:T(8,128)(2,1)S(1)}, bf16[256,256]{1,0:T(8,128)(2,1)S(1)}, u32[]{:S(2)}, u32[]{:S(2)}) collective-permute-start(bf16[256,256]{1,0:T(8,128)(2,1)S(1)} %get-tuple-element.29), channel_id=1, source_target_pairs={{0,3},{1,2},{2,1},{3,0},{4,7},{5,6},{6,5},{7,4},{8,11},{9,10},{10,... | collective-permute-start | bytes 393224 | tf_op jit(solution)/shard_map/ppermute | solution.py:27
  8.9 20.9 %collective-permute-start.8 = (bf16[256,256]{1,0:T(8,128)(2,1)S(1)}, bf16[256,256]{1,0:T(8,128)(2,1)S(1)}, u32[]{:S(2)}, u32[]{:S(2)}) collective-permute-start(bf16[256,256]{1,0:T(8,128)(2,1)S(1)} %get-tuple-element.29), channel_id=1, source_target_pairs={{0,2},{1,3},{2,0},{3,1},{4,6},{5,7},{6,4},{7,5},{8,10},{9,11},{10,... | collective-permute-start | bytes 393224 | tf_op jit(solution)/shard_map/ppermute | solution.py:27
  9.5 20.3 %collective-permute-start.7 = (bf16[256,256]{1,0:T(8,128)(2,1)S(1)}, bf16[256,256]{1,0:T(8,128)(2,1)S(1)}, u32[]{:S(2)}, u32[]{:S(2)}) collective-permute-start(bf16[256,256]{1,0:T(8,128)(2,1)S(1)} %get-tuple-element.29), channel_id=1, source_target_pairs={{0,1},{1,0},{2,3},{3,2},{4,5},{5,4},{6,7},{7,6},{8,9},{9,8},{10,11... | collective-permute-start | bytes 393224 | tf_op jit(solution)/shard_map/ppermute | solution.py:27
  29.9 26.0 %collective-permute-start.10 = (bf16[1024,256]{1,0:T(8,128)(2,1)S(1)}, bf16[1024,256]{1,0:T(8,128)(2,1)S(1)}, u32[]{:S(2)}, u32[]{:S(2)}) collective-permute-start(bf16[1024,256]{1,0:T(8,128)(2,1)S(1)} %pad_maximum_fusion.refs_0_), channel_id=1, source_target_pairs={{0,4},{4,0},{8,12},{12,8},{16,20},{20,16},{24,28},{28,24},{1,5},{5... | collective-permute-start | bytes 1572872 | tf_op jit(solution)/shard_map/ppermute | solution.py:27
  40.2 14.3 %collective-permute-start.6 = (s32[512]{0:T(512)}, s32[512]{0:T(512)}, u32[]{:S(2)}, u32[]{:S(2)}) collective-permute-start(s32[512]{0:T(512)} %concatenate.24), channel_id=1, source_target_pairs={{0,24},{4,28},{8,16},{12,20},{16,8},{20,12},{24,0},{28,4},{1,25},{... | collective-permute-start | bytes 6152 | tf_op jit(solution)/shard_map/ppermute | solution.py:27
  44.2 10.3 %collective-permute-start.5 = (s32[512]{0:T(512)}, s32[512]{0:T(512)}, u32[]{:S(2)}, u32[]{:S(2)}) collective-permute-start(s32[512]{0:T(512)} %concatenate.24), channel_id=1, source_target_pairs={{0,16},{4,20},{8,24},{12,28},{16,0},{20,4},{24,8},{28,12},{1,17},{... | collective-permute-start | bytes 6152 | tf_op jit(solution)/shard_map/ppermute | solution.py:27
  60.2 13.5 %collective-permute-start.11 = (bf16[1024,1024]{1,0:T(8,128)(2,1)}, bf16[1024,1024]{1,0:T(8,128)(2,1)S(1)}, u32[]{:S(2)}, u32[]{:S(2)}) collective-permute-start(bf16[1024,1024]{1,0:T(8,128)(2,1)} %get-tuple-element.18), channel_id=1, source_target_pairs={{0,4},{4,0},{8,12},{12,8},{16,20},{20,16},{24,28},{28,24},{1,5},{5... | collective-permute-start | bytes 6291464 | tf_op jit(solution)/shard_map/ppermute | solution.py:27
  60.2 9.2 %collective-permute-start.14 = (bf16[256,256]{1,0:T(8,128)(2,1)S(1)}, bf16[256,256]{1,0:T(8,128)(2,1)S(1)}, u32[]{:S(2)}, u32[]{:S(2)}) collective-permute-start(bf16[256,256]{1,0:T(8,128)(2,1)S(1)} %get-tuple-element.37), channel_id=1, source_target_pairs={{0,24},{4,28},{8,16},{12,20},{16,8},{20,12},{24,0},{28,4},{1,25},{... | collective-permute-start | bytes 393224 | tf_op jit(solution)/shard_map/ppermute | solution.py:27
  61.2 10.1 %collective-permute-start.13 = (bf16[256,256]{1,0:T(8,128)(2,1)S(1)}, bf16[256,256]{1,0:T(8,128)(2,1)S(1)}, u32[]{:S(2)}, u32[]{:S(2)}) collective-permute-start(bf16[256,256]{1,0:T(8,128)(2,1)S(1)} %get-tuple-element.37), channel_id=1, source_target_pairs={{0,8},{4,12},{8,0},{12,4},{16,24},{20,28},{24,16},{28,20},{1,9},{5... | collective-permute-start | bytes 393224 | tf_op jit(solution)/shard_map/ppermute | solution.py:27
  63.3 10.4 %collective-permute-start.12 = (bf16[256,256]{1,0:T(8,128)(2,1)S(1)}, bf16[256,256]{1,0:T(8,128)(2,1)S(1)}, u32[]{:S(2)}, u32[]{:S(2)}) collective-permute-start(bf16[256,256]{1,0:T(8,128)(2,1)S(1)} %get-tuple-element.37), channel_id=1, source_target_pairs={{0,16},{4,20},{8,24},{12,28},{16,0},{20,4},{24,8},{28,12},{1,17},{... | collective-permute-start | bytes 393224 | tf_op jit(solution)/shard_map/ppermute | solution.py:27
  77.3 31.7 %collective-permute-start.17 = (f32[1024,256]{1,0:T(8,128)}, f32[1024,256]{1,0:T(8,128)}, u32[]{:S(2)}, u32[]{:S(2)}) collective-permute-start(f32[1024,256]{1,0:T(8,128)} %fusion.75.refs_3_), channel_id=1, source_target_pairs={{0,4},{4,0},{8,12},{12,8},{16,20},{20,16},{24,28},{28,24},{1,5},{5... | collective-permute-start | bytes 3145736 | tf_op jit(solution)/shard_map/ppermute | solution.py:27
  81.2 14.8 %all-to-all-start.1 = ((f32[32,8,256]{2,1,0:T(8,128)}), f32[32,8,256]{2,1,0:T(8,128)S(1)}, u32[]{:S(2)}, u32[]{:S(2)}) async-start(f32[32,8,256]{2,1,0:T(8,128)} %bitcast.53), calls=%async_computation.1 | async-start | bytes 524288 | tf_op jit(solution)/shard_map/all_to_all | solution.py:39
  87.6 17.6 %collective-permute-start.15 = (f32[512,256]{1,0:T(8,128)}, f32[512,256]{1,0:T(8,128)S(1)}, u32[]{:S(2)}, u32[]{:S(2)}) collective-permute-start(f32[512,256]{1,0:T(8,128)} %convolution_add_fusion.2), channel_id=1, source_target_pairs={{0,8},{4,12},{8,0},{12,4},{16,24},{20,28},{24,16},{28,20},{1,9},{5... | collective-permute-start | bytes 1572872 | tf_op jit(solution)/shard_map/ppermute | solution.py:27
  96.7 17.3 %all-to-all-start.2 = ((f32[32,8,256]{2,1,0:T(8,128)}), f32[32,8,256]{2,1,0:T(8,128)S(1)}, u32[]{:S(2)}, u32[]{:S(2)}) async-start(f32[32,8,256]{2,1,0:T(8,128)} %broadcast_in_dim.8), calls=%async_computation.2 | async-start | bytes 524288 | tf_op jit(solution)/shard_map/all_to_all | solution.py:33
  105.3 13.8 %collective-permute-start.16 = (f32[256,256]{1,0:T(8,128)S(1)}, f32[256,256]{1,0:T(8,128)}, u32[]{:S(2)}, u32[]{:S(2)}) collective-permute-start(f32[256,256]{1,0:T(8,128)S(1)} %slice_add_fusion.4), channel_id=1, source_target_pairs={{0,16},{4,20},{8,24},{12,28},{16,0},{20,4},{24,8},{28,12},{1,17},{... | collective-permute-start | bytes 786440 | tf_op jit(solution)/shard_map/ppermute | solution.py:27
  110.5 9.4 %collective-permute-start.18 = (f32[256,256]{1,0:T(8,128)S(1)}, f32[256,256]{1,0:T(8,128)}, u32[]{:S(2)}, u32[]{:S(2)}) collective-permute-start(f32[256,256]{1,0:T(8,128)S(1)} %get-tuple-element.34), channel_id=1, source_target_pairs={{0,1},{1,0},{2,3},{3,2},{4,5},{5,4},{6,7},{7,6},{8,9},{9,8},{10,11... | collective-permute-start | bytes 786440 | tf_op jit(solution)/shard_map/ppermute | solution.py:27
  111.2 13.0 %collective-permute-start.20 = (f32[256,256]{1,0:T(8,128)S(1)}, f32[256,256]{1,0:T(8,128)}, u32[]{:S(2)}, u32[]{:S(2)}) collective-permute-start(f32[256,256]{1,0:T(8,128)S(1)} %get-tuple-element.35), channel_id=1, source_target_pairs={{0,3},{1,2},{2,1},{3,0},{4,7},{5,6},{6,5},{7,4},{8,11},{9,10},{10,... | collective-permute-start | bytes 786440 | tf_op jit(solution)/shard_map/ppermute | solution.py:27
  113.6 12.1 %collective-permute-start.19 = (f32[256,256]{1,0:T(8,128)S(1)}, f32[256,256]{1,0:T(8,128)}, u32[]{:S(2)}, u32[]{:S(2)}) collective-permute-start(f32[256,256]{1,0:T(8,128)S(1)} %get-tuple-element.36), channel_id=1, source_target_pairs={{0,2},{1,3},{2,0},{3,1},{4,6},{5,7},{6,4},{7,5},{8,10},{9,11},{10,... | collective-permute-start | bytes 786440 | tf_op jit(solution)/shard_map/ppermute | solution.py:27
  145.5 14.4 %collective-permute-start.24 = (bf16[1024,256]{1,0:T(8,128)(2,1)S(1)}, bf16[1024,256]{1,0:T(8,128)(2,1)S(1)}, u32[]{:S(2)}, u32[]{:S(2)}) collective-permute-start(bf16[1024,256]{1,0:T(8,128)(2,1)S(1)} %pad_maximum_fusion.2.refs_0_), channel_id=1, source_target_pairs={{0,4},{4,0},{8,12},{12,8},{16,20},{20,16},{24,28},{28,24},{1,5},{5... | collective-permute-start | bytes 1572872 | tf_op jit(solution)/shard_map/ppermute | solution.py:27
  146.4 9.2 %collective-permute-start.27 = (bf16[256,256]{1,0:T(8,128)(2,1)S(1)}, bf16[256,256]{1,0:T(8,128)(2,1)S(1)}, u32[]{:S(2)}, u32[]{:S(2)}) collective-permute-start(bf16[256,256]{1,0:T(8,128)(2,1)S(1)} %fusion.69), channel_id=1, source_target_pairs={{0,24},{4,28},{8,16},{12,20},{16,8},{20,12},{24,0},{28,4},{1,25},{... | collective-permute-start | bytes 393224 | tf_op jit(solution)/shard_map/ppermute | solution.py:27
  147.1 9.4 %collective-permute-start.26 = (bf16[256,256]{1,0:T(8,128)(2,1)S(1)}, bf16[256,256]{1,0:T(8,128)(2,1)S(1)}, u32[]{:S(2)}, u32[]{:S(2)}) collective-permute-start(bf16[256,256]{1,0:T(8,128)(2,1)S(1)} %fusion.69), channel_id=1, source_target_pairs={{0,8},{4,12},{8,0},{12,4},{16,24},{20,28},{24,16},{28,20},{1,9},{5... | collective-permute-start | bytes 393224 | tf_op jit(solution)/shard_map/ppermute | solution.py:27
  148.8 11.1 %collective-permute-start.25 = (bf16[256,256]{1,0:T(8,128)(2,1)S(1)}, bf16[256,256]{1,0:T(8,128)(2,1)S(1)}, u32[]{:S(2)}, u32[]{:S(2)}) collective-permute-start(bf16[256,256]{1,0:T(8,128)(2,1)S(1)} %fusion.69), channel_id=1, source_target_pairs={{0,16},{4,20},{8,24},{12,28},{16,0},{20,4},{24,8},{28,12},{1,17},{... | collective-permute-start | bytes 393224 | tf_op jit(solution)/shard_map/ppermute | solution.py:27
  164.3 31.1 %collective-permute-start.28 = (f32[1024,256]{1,0:T(8,128)}, f32[1024,256]{1,0:T(8,128)}, u32[]{:S(2)}, u32[]{:S(2)}) collective-permute-start(f32[1024,256]{1,0:T(8,128)} %fusion.77.refs_3_), channel_id=1, source_target_pairs={{0,4},{4,0},{8,12},{12,8},{16,20},{20,16},{24,28},{28,24},{1,5},{5... | collective-permute-start | bytes 3145736 | tf_op jit(solution)/shard_map/ppermute | solution.py:27
  168.1 13.6 %all-to-all-start.4 = ((f32[32,8,256]{2,1,0:T(8,128)}), f32[32,8,256]{2,1,0:T(8,128)S(1)}, u32[]{:S(2)}, u32[]{:S(2)}) async-start(f32[32,8,256]{2,1,0:T(8,128)} %bitcast.52), calls=%async_computation.4 | async-start | bytes 524288 | tf_op jit(solution)/shard_map/all_to_all | solution.py:39
  173.3 17.6 %collective-permute-start.32 = (f32[512,256]{1,0:T(8,128)}, f32[512,256]{1,0:T(8,128)S(1)}, u32[]{:S(2)}, u32[]{:S(2)}) collective-permute-start(f32[512,256]{1,0:T(8,128)} %convolution_add_fusion.1), channel_id=1, source_target_pairs={{0,8},{4,12},{8,0},{12,4},{16,24},{20,28},{24,16},{28,20},{1,9},{5... | collective-permute-start | bytes 1572872 | tf_op jit(solution)/shard_map/ppermute | solution.py:27
  182.5 22.9 %all-to-all-start.5 = ((f32[32,8,256]{2,1,0:T(8,128)}), f32[32,8,256]{2,1,0:T(8,128)S(1)}, u32[]{:S(2)}, u32[]{:S(2)}) async-start(f32[32,8,256]{2,1,0:T(8,128)} %broadcast_in_dim.10), calls=%async_computation.5 | async-start | bytes 524288 | tf_op jit(solution)/shard_map/all_to_all | solution.py:33
  191.6 13.8 %collective-permute-start.33 = (f32[256,256]{1,0:T(8,128)S(1)}, f32[256,256]{1,0:T(8,128)}, u32[]{:S(2)}, u32[]{:S(2)}) collective-permute-start(f32[256,256]{1,0:T(8,128)S(1)} %slice_add_fusion), channel_id=1, source_target_pairs={{0,16},{4,20},{8,24},{12,28},{16,0},{20,4},{24,8},{28,12},{1,17},{... | collective-permute-start | bytes 786440 | tf_op jit(solution)/shard_map/ppermute | solution.py:27
  196.8 10.1 %collective-permute-start.29 = (f32[256,256]{1,0:T(8,128)S(1)}, f32[256,256]{1,0:T(8,128)S(1)}, u32[]{:S(2)}, u32[]{:S(2)}) collective-permute-start(f32[256,256]{1,0:T(8,128)S(1)} %get-tuple-element.31), channel_id=1, source_target_pairs={{0,1},{1,0},{2,3},{3,2},{4,5},{5,4},{6,7},{7,6},{8,9},{9,8},{10,11... | collective-permute-start | bytes 786440 | tf_op jit(solution)/shard_map/ppermute | solution.py:27
  197.6 12.9 %collective-permute-start.31 = (f32[256,256]{1,0:T(8,128)S(1)}, f32[256,256]{1,0:T(8,128)}, u32[]{:S(2)}, u32[]{:S(2)}) collective-permute-start(f32[256,256]{1,0:T(8,128)S(1)} %get-tuple-element.32), channel_id=1, source_target_pairs={{0,3},{1,2},{2,1},{3,0},{4,7},{5,6},{6,5},{7,4},{8,11},{9,10},{10,... | collective-permute-start | bytes 786440 | tf_op jit(solution)/shard_map/ppermute | solution.py:27
  200.0 11.9 %collective-permute-start.30 = (f32[256,256]{1,0:T(8,128)S(1)}, f32[256,256]{1,0:T(8,128)}, u32[]{:S(2)}, u32[]{:S(2)}) collective-permute-start(f32[256,256]{1,0:T(8,128)S(1)} %get-tuple-element.33), channel_id=1, source_target_pairs={{0,2},{1,3},{2,0},{3,1},{4,6},{5,7},{6,4},{7,5},{8,10},{9,11},{10,... | collective-permute-start | bytes 786440 | tf_op jit(solution)/shard_map/ppermute | solution.py:27
  213.9 8.8 %all-to-all-start.6 = ((f32[32,2,256]{2,1,0:T(2,128)}), f32[32,2,256]{2,1,0:T(2,128)S(1)}, u32[]{:S(2)}, u32[]{:S(2)}) async-start(f32[32,2,256]{2,1,0:T(2,128)} %broadcast_in_dim.11), calls=%async_computation.6 | async-start | bytes 131072 | tf_op jit(solution)/shard_map/all_to_all | solution.py:33
  (44 other events, 461.7 us)
